TPU v7x, 32 devices: a whole 2x2x4 slice. The times are simulated.
32 devices in a mesh: groups: 1, px: 16 (over z, y, x), py: 2 (over core).
Axes of the slice: x: 2, y: 2, z: 4, core: 2. Of those that a mesh axis runs over, the one named last changes fastest.
Arguments:
- field: bfloat16 [1, 20, 384, 192, 128], P('groups', None, 'px', 'py'), may hold values from -6 to 6
- spectral_weight: bfloat16 [2, 20, 20, 1536, 96], P(None, None, None, ('py', 'px')), may hold values from -6 to 6
- pointwise_weight: bfloat16 [20, 20], replicated, may hold values from -1.25 to 1.25
- bias: float32 [20], replicated, may hold values from -3 to 3
Outputs:
- mixed_field: bfloat16 [1, 20, 384, 192, 128], P('groups', None, 'px', 'py')
All inputs are finite; a program needn't handle non-finite values.
Results may differ from a plain program's by a relative error of at most 0.001.
Values sent between devices are 32-bit elements; how exact they have to be, the bound alone decides.
A program may use at most 192 MiB of HBM per device.

v0:
```python
import jax
import jax.numpy as jnp
from jax import lax
from jax.sharding import PartitionSpec as P

NX = 384
NY = 192
NZ = 128
MX = 96
MY = 48
MZ = 32


PRECISION_HIGH = lax.Precision.HIGHEST
TWO_PI = 6.283185307179586


def kept_frequency(length, retained):
    index = jnp.arange(retained, dtype=jnp.int32)
    return jnp.where(index < retained // 2, index, length - retained + index)


def phases(frequency, positions, length):
    product = frequency[:, None] * positions[None, :] % length
    return product.astype(jnp.float32) * (TWO_PI / length)


def forward_table(length, retained, positions):
    angle = phases(kept_frequency(length, retained), positions, length).T
    cosine = jnp.cos(angle)
    sine_part = jnp.sin(angle)
    rows_real = jnp.stack([cosine, -sine_part], 1)
    rows_imag = jnp.stack([sine_part, cosine], 1)
    return jnp.stack([rows_real, rows_imag], 1)


def inverse_table(length, retained, positions):
    angle = phases(kept_frequency(length, retained), positions, length)
    cosine = jnp.cos(angle)
    sine_part = jnp.sin(angle)
    rows_real = jnp.stack([cosine, sine_part], 1)
    rows_imag = jnp.stack([-sine_part, cosine], 1)
    return jnp.stack([rows_real, rows_imag], 1)


def mix_modes(weight_part, values):
    return jnp.einsum("iomk,bimk->bomk", weight_part, values, precision=PRECISION_HIGH)


def per_device(field, spectral_weight, pointwise_weight, bias):
    samples, channels, x_local, y_local, z_cells = field.shape
    y_devices = lax.axis_size("py")
    z_modes_local = MZ // y_devices
    y_start = lax.axis_index("py") * y_local
    own_rows = y_start + jnp.arange(y_local, dtype=jnp.int32)
    z_phase = phases(jnp.arange(MZ, dtype=jnp.int32), jnp.arange(NZ, dtype=jnp.int32), NZ)
    z_forward = jnp.stack([jnp.cos(z_phase), -jnp.sin(z_phase)], 0)
    z_hat = jnp.einsum(
        "bcxyz,skz->bcxsky", field.astype(jnp.float32), z_forward, precision=PRECISION_HIGH
    )
    y_whole = lax.all_to_all(z_hat, "py", split_axis=4, concat_axis=5, tiled=True)
    y_table = forward_table(NY, MY, jnp.arange(NY, dtype=jnp.int32))
    y_hat = jnp.einsum("bcxrky,yrsq->bcxskq", y_whole, y_table, precision=PRECISION_HIGH)
    flat_modes = y_hat.reshape(samples, channels, x_local, 2, z_modes_local * MY)
    x_table = forward_table(NX, MX, jnp.arange(NX, dtype=jnp.int32))
    x_back = inverse_table(NX, MX, jnp.arange(NX, dtype=jnp.int32))
    weight_real = spectral_weight[0].astype(jnp.float32)
    weight_imag = spectral_weight[1].astype(jnp.float32)
    spectrum = jnp.einsum(
        "bcxrm,xrsk->bcsmk",
        lax.all_to_all(flat_modes, "px", split_axis=4, concat_axis=2, tiled=True),
        x_table,
        precision=PRECISION_HIGH,
    )
    real_in = spectrum[:, :, 0]
    imag_in = spectrum[:, :, 1]
    real_out = mix_modes(weight_real, real_in) - mix_modes(weight_imag, imag_in)
    imag_out = mix_modes(weight_real, imag_in) + mix_modes(weight_imag, real_in)
    mixed = jnp.stack([real_out, imag_out], 2)
    spatial = jnp.einsum("bcrmk,krsx->bcxsm", mixed, x_back, precision=PRECISION_HIGH)
    returned = lax.all_to_all(spatial, "px", split_axis=2, concat_axis=4, tiled=True)
    returned = returned.reshape(samples, channels, x_local, 2, z_modes_local, MY)
    own_back = inverse_table(NY, MY, own_rows)
    z_ready = jnp.einsum(
        "bcxrkq,qrsy->bcxsky",
        lax.all_gather(returned, "py", axis=4, tiled=True),
        own_back,
        precision=PRECISION_HIGH,
    )
    weighting = jnp.where(jnp.arange(MZ) == 0, 1.0, 2.0).astype(jnp.float32) / float(NX * NY * NZ)
    z_inverse = jnp.stack(
        [jnp.cos(z_phase) * weighting[:, None], -jnp.sin(z_phase) * weighting[:, None]], 0
    )
    spectral = jnp.einsum("bcxsky,skz->bcxyz", z_ready, z_inverse, precision=PRECISION_HIGH)
    mixing_rows = pointwise_weight.T
    local_part = jnp.dot(
        mixing_rows, field[0].reshape(channels, -1), preferred_element_type=jnp.float32
    )
    local_part = local_part.reshape(channels, x_local, y_local, z_cells)
    total = spectral[0] + local_part + bias[:, None, None, None]
    outputs = [jax.nn.gelu(total).astype(jnp.bfloat16)]
    return jnp.stack(outputs)


def solution(mesh):
    in_specs = (
        P("groups", None, "px", "py", None),
        P(None, None, None, ("py", "px"), None),
        P(),
        P(),
    )
    out_specs = P("groups", None, "px", "py", None)
    return jax.shard_map(
        per_device, mesh=mesh, in_specs=in_specs, out_specs=out_specs, check_vma=False
    )
```

profile of v0, /device:TPU:0, one launch (start us, length us, event | category | flops | bytes accessed | tf_op | source)
XLA Modules:
  0.0 632.7 jit_solution(357106362431477268)
XLA Ops:
  6.6 31.2 %fusion.22 = f32[1,20,24,2,32,96]{5,4,2,1,3,0:T(8,128)} fusion(bf16[1,20,24,96,128]{4,3,2,1,0:T(8,128)(2,1)} %param.4, f32[1,32,128]{2,1,0:T(8,128)S(1)} %get-tuple-element.35, f32[1,32,128]{2,1,0:T(8,128)S(1)} %get-tuple-element.36), kind=kOutput, calls=%fused_computation.30 | convolution fusion | flops 4529856512 | bytes 23625728 | tf_op jit(solution)/shard_map/bcxyz,skz->bcxsky/dot_general | solution.py:58
  37.8 20.1 %copy.51 = f32[1,20,24,2,32,96]{5,2,1,3,0,4:T(8,128)} copy(f32[1,20,24,2,32,96]{5,4,2,1,3,0:T(8,128)} %fusion.22) | data formatting | bytes 23592960 | tf_op jit(solution)/shard_map/bcxyz,skz->bcxsky/transpose | solution.py:58
  57.9 9.3 %all-to-all-start = ((f32[1,20,24,2,32,96]{5,2,1,3,0,4:T(8,128)}), f32[1,20,24,2,32,96]{5,2,1,3,0,4:T(8,128)}, u32[]{:S(2)}, u32[]{:S(2)}) async-start(f32[1,20,24,2,32,96]{5,2,1,3,0,4:T(8,128)} %copy.51), calls=%async_computation | async-start | bytes 31457280 | tf_op jit(solution)/shard_map/all_to_all | solution.py:61
  67.6 12.5 %all-to-all-done = f32[1,20,24,2,32,96]{5,2,1,3,0,4:T(8,128)} async-done(((f32[1,20,24,2,32,96]{5,2,1,3,0,4:T(8,128)}), f32[1,20,24,2,32,96]{5,2,1,3,0,4:T(8,128)}, u32[]{:S(2)}, u32[]{:S(2)}) %all-to-all-start) | async-done | bytes 11796512 | tf_op jit(solution)/shard_map/all_to_all | solution.py:61
  80.1 27.4 %copy.129 = f32[1,20,24,2,2,16,96]{6,4,2,3,5,1,0:T(2,128)} copy(f32[1,20,24,2,2,16,96]{6,2,1,3,5,4,0:T(8,128)} %bitcast.34) | data formatting | bytes 23592960 | tf_op jit(solution)/shard_map/all_to_all | solution.py:61
  107.5 19.4 %reshape.676 = f32[20,24,2,16,192,1]{4,1,2,3,0,5:T(8,128)} reshape(f32[1,20,24,2,16,2,96]{6,5,2,3,4,1,0:T(2,128)} %bitcast.186) | data formatting | bytes 23592960 | tf_op jit(solution)/shard_map/reshape.2
  126.9 17.4 %convolution_bitcast_fusion = f32[1,20,24,2,16,48]{5,2,4,1,3,0:T(8,128)} fusion(f32[20,24,2,16,192,1]{4,1,2,3,0,5:T(8,128)} %reshape.676, f32[192,1,2,48]{0,3,1,2:T(8,128)S(1)} %get-tuple-element.18, f32[192,1,2,48]{0,3,1,2:T(8,128)S(1)} %get-tuple-element.17), kind=kOutput, calls=%fused_computation.32 | convolution fusion | flops 3397423104 | bytes 14893056 | tf_op jit(solution)/shard_map/bcxrky,yrsq->bcxskq/dot_general | solution.py:63
  144.3 19.3 %copy.106 = f32[1,20,24,2,16,48]{2,3,1,5,4,0:T(2,128)} copy(f32[1,20,24,2,16,48]{5,2,4,1,3,0:T(8,128)} %convolution_bitcast_fusion) | data formatting | bytes 5898240 | tf_op jit(solution)/shard_map/reshape | solution.py:64
  163.5 29.7 %reshape.699 = f32[16,1,46080]{2,1,0:T(1,128)} reshape(f32[768,1,20,2,24]{4,3,2,1,0:T(2,128)} %bitcast.187) | data formatting | bytes 5898240
  193.3 8.3 %all-to-all-start.1 = ((f32[16,1,46080]{2,1,0:T(1,128)}), f32[16,1,46080]{2,1,0:T(1,128)S(1)}, u32[]{:S(2)}, u32[]{:S(2)}) async-start(f32[16,1,46080]{2,1,0:T(1,128)} %reshape.699), calls=%async_computation.1 | async-start | bytes 5898240 | tf_op jit(solution)/shard_map/all_to_all | solution.py:71
  203.5 0.9 maximum_bitcast_fusion.8
  204.3 54.9 %all-to-all-done.1 = f32[16,1,46080]{2,1,0:T(1,128)S(1)} async-done(((f32[16,1,46080]{2,1,0:T(1,128)}), f32[16,1,46080]{2,1,0:T(1,128)S(1)}, u32[]{:S(2)}, u32[]{:S(2)}) %all-to-all-start.1) | async-done | bytes 2949152 | tf_op jit(solution)/shard_map/all_to_all | solution.py:71
  259.3 1.6 copy-done.1
  261.5 9.8 %reduce.8 = f32[16,46080]{1,0:T(8,128)S(1)} reduce(f32[16,1,46080]{2,1,0:T(1,128)} %copy-done.1, f32[]{:T(128)} %broadcast.792), dimensions={1}, to_apply=%all_to_all.36.reduce_sub_computation | reduce | bytes 5898244 | tf_op jit(solution)/shard_map/all_to_all | solution.py:71
  271.2 31.9 %reshape.700 = f32[768,1,20,2,24]{4,3,2,1,0:T(2,128)} reshape(f32[16,46080]{1,0:T(8,128)S(1)} %reduce.8) | data formatting | bytes 5898240
  303.2 19.5 %copy.108 = f32[1,20,24,2,16,48]{5,2,4,3,1,0:T(8,128)} copy(f32[1,20,24,2,16,48]{2,3,1,5,4,0:T(2,128)} %bitcast.188) | data formatting | bytes 5898240 | tf_op jit(solution)/shard_map/all_to_all | solution.py:71
  322.6 15.1 %convolution_bitcast_fusion.2 = f32[1,20,2,48,96]{4,3,1,2,0:T(8,128)S(1)} fusion(f32[20,384,2,48,1]{3,1,2,0,4:T(8,128)} %bitcast.193, f32[384,1,2,96]{0,3,1,2:T(8,128)S(1)} %copy-done.3, f32[384,1,2,96]{0,3,1,2:T(8,128)S(1)} %copy-done.2), kind=kOutput, calls=%fused_computation.34 | convolution fusion | flops 1698840576 | bytes 4276224 | tf_op jit(solution)/shard_map/bcxrm,xrsk->bcsmk/dot_general | solution.py:69
  337.8 7.2 %fusion.20 = (f32[48,96,20]{1,0,2:T(8,128)S(1)}, f32[48,96,20]{1,0,2:T(8,128)S(1)}, f32[48,96,20]{1,0,2:T(8,128)S(1)}, f32[48,96,20]{1,0,2:T(8,128)S(1)}) fusion(f32[48,96,20]{1,0,2:T(8,128)S(1)} %get-tuple-element.12, bf16[2,20,20,48,96]{4,3,2,1,0:T(8,128)(2,1)} %param.5, f32[48,96,20]{1,0,2:T(8,128)S(1)} %get-tuple-element.11), kind=kLoop, calls=%fused_computation.27 | loop fusion | flops 18063360 | bytes 9584640 | tf_op jit(solution)/shard_map/iomk,bimk->bomk/dot_general | solution.py:47
  345.2 2.7 convolution_bitcast_fusion.1
  347.9 6.8 %copy.58 = f32[1,20,384,2,48]{4,3,1,0,2:T(2,128)} copy(f32[1,20,384,2,48]{2,4,1,3,0:T(8,128)S(1)} %convolution_bitcast_fusion.1) | data formatting | bytes 5898240 | tf_op jit(solution)/shard_map/bcrmk,krsx->bcxsm/transpose | solution.py:80
  354.7 15.2 %reshape.701 = f32[16,1,46080]{2,1,0:T(1,128)} reshape(f32[384,1,20,2,48]{4,3,2,1,0:T(2,128)} %bitcast.194) | data formatting | bytes 5898240
  369.9 81.5 %all_to_all.45 = f32[16,1,46080]{2,1,0:T(1,128)S(1)} all-to-all(f32[16,1,46080]{2,1,0:T(1,128)} %reshape.701), channel_id=1, replica_groups=mesh['groups'=1,'px'=16,'py'=2] {'px'}, dimensions={0} | all-to-all | bytes 5898240 | tf_op jit(solution)/shard_map/all_to_all | solution.py:81
  451.4 10.2 %reduce.9 = f32[16,46080]{1,0:T(8,128)} reduce(f32[16,1,46080]{2,1,0:T(1,128)S(1)} %all_to_all.45, f32[]{:T(128)} %broadcast.792), dimensions={1}, to_apply=%all_to_all.39.reduce_sub_computation | reduce | bytes 5898244 | tf_op jit(solution)/shard_map/all_to_all | solution.py:81
  461.7 16.1 %reshape.702 = f32[384,1,20,2,48]{4,3,2,1,0:T(2,128)} reshape(f32[16,46080]{1,0:T(8,128)} %reduce.9) | data formatting | bytes 5898240
  477.8 10.9 %copy.130 = f32[1,20,16,24,2,48]{5,2,4,3,1,0:T(8,128)} copy(f32[1,20,16,24,2,48]{5,4,1,3,2,0:T(2,128)} %bitcast.195) | data formatting | bytes 5898240 | tf_op jit(solution)/shard_map/all_to_all | solution.py:81
  488.7 22.0 %reshape_squeeze.3 = bf16[20,294912]{1,0:T(8,128)(2,1)} reshape(bf16[1,20,24,96,128]{4,3,2,1,0:T(8,128)(2,1)} %param.4) | data formatting | bytes 23592960 | tf_op jit(solution)/shard_map/reshape;squeeze | solution.py:97
  510.7 8.6 %copy.116 = bf16[3,8,2304,128]{3,2,1,0:T(8,128)(2,1)S(1)} copy(bf16[3,8,2304,128]{3,1,2,0:T(8,128)(2,1)} %bitcast.190) | data formatting | bytes 28311552
  519.3 5.5 slice.18
  525.1 20.0 %fusion.13 = f32[20,24,96,128]{3,0,2,1:T(8,128)} fusion(bf16[24,96,128,20]{2,1,0,3:T(8,128)(2,1)} %bitcast.189, bf16[20,20]{1,0:T(8,128)(2,1)S(1)} %copy-done), kind=kOutput, calls=%fused_computation.16 | convolution fusion | flops 235929600 | bytes 35390240 | tf_op jit(solution)/shard_map/dot_general | solution.py:96
  545.2 20.9 %fusion.25 = f32[20,24,2,32,96]{4,3,1,0,2:T(8,128)} fusion(f32[1,20,24,2,32,48]{5,4,3,2,1,0:T(8,128)} %all-gather.2.cloned.1.call-done, f32[48,1,2,96]{3,0,1,2:T(8,128)S(1)} %get-tuple-element.20, f32[48,1,2,96]{3,0,1,2:T(8,128)S(1)} %get-tuple-element.19), kind=kOutput, calls=%fused_computation.31 | convolution fusion | flops 3397404672 | bytes 17768448 | tf_op jit(solution)/shard_map/bcxrkq,qrsy->bcxsky/dot_general | solution.py:84
  566.1 42.4 %fusion.11 = f32[20,24,96,128,1]{3,2,0,1,4:T(8,128)} fusion(f32[20,24,2,32,96]{4,3,1,0,2:T(8,128)} %fusion.25, f32[1,32,128]{2,1,0:T(8,128)S(1)} %get-tuple-element.25, f32[1,32,128]{2,1,0:T(8,128)S(1)} %get-tuple-element.24), kind=kOutput, calls=%fused_computation.13 | convolution fusion | flops 4529856512 | bytes 35422208 | tf_op jit(solution)/shard_map/bcxsky,skz->bcxyz/dot_general | solution.py:94
  608.6 16.8 %fusion.17 = bf16[1,20,24,96,128]{4,3,2,1,0:T(8,128)(2,1)} fusion(f32[20]{0:T(128)S(1)} %copy-done.4, f32[20,24,96,128]{3,0,2,1:T(8,128)S(1)} %bitcast.185, f32[20,24,96,128,1]{3,2,0,1,4:T(8,128)} %fusion.11), kind=kLoop, calls=%fused_computation.24 | loop fusion | flops 64880640 | bytes 58982480 | tf_op jit(solution)/shard_map/stack | solution.py:102
  (44 shorter events, 3.4 us)
Async XLA Ops:
  6.5 518.6 %copy-start = (bf16[20,20]{1,0:T(8,128)(2,1)S(1)}, bf16[20,20]{1,0:T(8,128)(2,1)}, u32[]{:S(2)}) copy-start(bf16[20,20]{1,0:T(8,128)(2,1)} %param.6) | copy-start | bytes 2404
  57.9 22.2 %all-to-all-start = ((f32[1,20,24,2,32,96]{5,2,1,3,0,4:T(8,128)}), f32[1,20,24,2,32,96]{5,2,1,3,0,4:T(8,128)}, u32[]{:S(2)}, u32[]{:S(2)}) async-start(f32[1,20,24,2,32,96]{5,2,1,3,0,4:T(8,128)} %copy.51), calls=%async_computation | async-start | bytes 31457280 | tf_op jit(solution)/shard_map/all_to_all | solution.py:61
  193.3 66.0 %all-to-all-start.1 = ((f32[16,1,46080]{2,1,0:T(1,128)}), f32[16,1,46080]{2,1,0:T(1,128)S(1)}, u32[]{:S(2)}, u32[]{:S(2)}) async-start(f32[16,1,46080]{2,1,0:T(1,128)} %reshape.699), calls=%async_computation.1 | async-start | bytes 5898240 | tf_op jit(solution)/shard_map/all_to_all | solution.py:71
  201.6 343.6 %all-gather.2.cloned.1.call-start = ((), (), s32[]{:S(2)}) async-start(), calls=%async_computation.3 | async-start | bytes 23592960 | tf_op jit(solution)/shard_map/all_gather | solution.py:86
  259.3 1.6 copy-start.1
  303.1 19.5 %copy-start.2 = (f32[384,1,2,96]{0,3,1,2:T(8,128)S(1)}, f32[384,1,2,96]{0,3,1,2:T(8,128)}, u32[]{:S(2)}) copy-start(f32[384,1,2,96]{0,3,1,2:T(8,128)} %get-tuple-element.15) | copy-start | bytes 884740
  303.1 19.5 %copy-start.3 = (f32[384,1,2,96]{0,3,1,2:T(8,128)S(1)}, f32[384,1,2,96]{0,3,1,2:T(8,128)}, u32[]{:S(2)}) copy-start(f32[384,1,2,96]{0,3,1,2:T(8,128)} %get-tuple-element.16) | copy-start | bytes 884740
  545.2 63.3 %slice-start = ((s8[28311552]{0:T(1024)(128)(4,1)}), s8[4194304]{0:T(1024)(128)(4,1)S(1)}, s32[]{:S(2)}) async-start(s8[28311552]{0:T(1024)(128)(4,1)} %bitcast.184), calls=%async_computation.4 | async-start | bytes 8388608
  545.2 63.3 %slice-start.1 = ((s8[28311552]{0:T(1024)(128)(4,1)}), s8[4194304]{0:T(1024)(128)(4,1)S(1)}, s32[]{:S(2)}) async-start(s8[28311552]{0:T(1024)(128)(4,1)} %bitcast.184), calls=%async_computation.5 | async-start | bytes 8388608
  545.2 63.3 %slice-start.2 = ((s8[28311552]{0:T(1024)(128)(4,1)}), s8[4194304]{0:T(1024)(128)(4,1)S(1)}, s32[]{:S(2)}) async-start(s8[28311552]{0:T(1024)(128)(4,1)} %bitcast.184), calls=%async_computation.6 | async-start | bytes 8388608
  545.2 63.3 %slice-start.3 = ((s8[28311552]{0:T(1024)(128)(4,1)}), s8[4194304]{0:T(1024)(128)(4,1)S(1)}, s32[]{:S(2)}) async-start(s8[28311552]{0:T(1024)(128)(4,1)} %bitcast.184), calls=%async_computation.7 | async-start | bytes 8388608
  566.1 42.4 %slice-start.4 = ((s8[28311552]{0:T(1024)(128)(4,1)}), s8[4194304]{0:T(1024)(128)(4,1)S(1)}, s32[]{:S(2)}) async-start(s8[28311552]{0:T(1024)(128)(4,1)} %bitcast.184), calls=%async_computation.8 | async-start | bytes 8388608
  566.1 42.4 %slice-start.5 = ((s8[28311552]{0:T(1024)(128)(4,1)}), s8[4194304]{0:T(1024)(128)(4,1)S(1)}, s32[]{:S(2)}) async-start(s8[28311552]{0:T(1024)(128)(4,1)} %bitcast.184), calls=%async_computation.9 | async-start | bytes 8388608
  566.1 42.4 %slice-start.6 = ((s8[28311552]{0:T(1024)(128)(4,1)}), s8[3145728]{0:T(1024)(128)(4,1)S(1)}, s32[]{:S(2)}) async-start(s8[28311552]{0:T(1024)(128)(4,1)} %bitcast.184), calls=%async_computation.10 | async-start | bytes 6291456
  566.1 42.4 %copy-start.4 = (f32[20]{0:T(128)S(1)}, f32[20]{0:T(128)}, u32[]{:S(2)}) copy-start(f32[20]{0:T(128)} %param.7) | copy-start | bytes 244
Sparse Core Ops, SparseCore 0:
  488.9 26.5 all-gather.1
where the time goes:
time: 640 us; the launch traced here: 633 us
  local copies, waits for them, and re-layouts  255 us (40%)
  matrix products  150 us (23%)
  blocking collectives  81.5 us (13%)
  waiting for transfers between devices  67.5 us (11%)
  other arithmetic  47 us (7%)
  starting transfers between devices  18.1 us (3%)
  between operations  14.1 us (2%)
    unnamed x31, local copies, waits for them, and re-layouts  109 us
    all_to_all x1, blocking collectives, per_device(): lax.all_to_all(spatial, 'px', split_axis=2, concat_axis=4, tiled=True)  81.5 us
    all_to_all x1, waiting for transfers between devices, per_device(): lax.all_to_all(flat_modes, 'px', split_axis=4, concat_axis=2, tiled=True)  54.9 us
    dot_general x1, matrix products, per_device(): jnp.einsum('bcxsky,skz->bcxyz', z_ready, z_inverse, precision=PRECISION_H...  42.4 us
    dot_general x1, matrix products, per_device(): jnp.einsum('bcxyz,skz->bcxsky', field.astype(jnp.float32), z_forward, pre...  31.2 us
    all_to_all x1, local copies, waits for them, and re-layouts, per_device(): lax.all_to_all(z_hat, 'py', split_axis=4, concat_axis=5, tiled=True)  27.4 us
    another operation x1, local copies, waits for them, and re-layouts, per_device(): field[0].reshape(channels, -1)  22 us
    dot_general x1, matrix products, per_device(): jnp.einsum('bcxrkq,qrsy->bcxsky', lax.all_gather(returned, 'py', axis=4,...  20.9 us
  transfers between devices with their start and end apart: 3, of which 2 were waited for; matrix products, arithmetic and copies ran while one was open for 9% of the time, Pallas kernels for 0%

commit v1 on v0

v1 whole, which is shorter than its diff:
```python
import functools

import jax
import jax.numpy as jnp
import numpy as np
from jax import lax
from jax.experimental import pallas as pl
from jax.experimental.pallas import tpu as pltpu
from jax.sharding import PartitionSpec as P

BF16 = jnp.bfloat16
F32 = jnp.float32


def kept(length, retained):
    index = np.arange(retained)
    return np.where(index < retained // 2, index, length - retained + index)


def angles(frequency, positions, length):
    return 2 * np.pi * (np.outer(frequency, positions) % length) / length


def split_np(table):
    high = table.astype(np.float32).astype(BF16)
    low = (table - high.astype(np.float64)).astype(np.float32).astype(BF16)
    return high, low


def split(values):
    high = values.astype(BF16)
    return high, (values - high.astype(F32)).astype(BF16)


def dot(a, b):
    return jnp.dot(a, b, preferred_element_type=F32)


def dot_nt(a, b):
    return lax.dot_general(a, b, (((1,), (1,)), ((), ())), preferred_element_type=F32)


def dot_tn(a, b):
    return lax.dot_general(a, b, (((0,), (0,)), ((), ())), preferred_element_type=F32)


def forward_kernel(direct, my, field_ref, t_ref, z_ref, own_ref, other_ref, g_high, g_low):
    channels, _, _, nz = field_ref.shape
    used, held = channels * my, g_high.shape[0]
    step = pl.program_id(0) * pl.num_programs(1) + pl.program_id(1)

    if held > used:
        @pl.when(step == 0)
        def _():
            g_high[used:] = jnp.zeros((held - used, 2 * nz), BF16)
            g_low[used:] = jnp.zeros((held - used, 2 * nz), BF16)

    table = t_ref[...]
    for c in range(channels):
        cells = field_ref[c, 0]
        high, low = split(dot(table, jnp.concatenate([cells, cells], 0)))
        rows = slice(c * my, (c + 1) * my)
        for q in range(2):
            g_high[rows, q * nz:(q + 1) * nz] = high[q * my:(q + 1) * my]
            g_low[rows, q * nz:(q + 1) * nz] = low[q * my:(q + 1) * my]
    modes = z_ref.shape[0] // 2
    first = dot_nt(z_ref[...], g_high[...])
    out = first[:modes] + first[modes:] + dot_nt(z_ref[:modes], g_low[...])
    half = modes // 2
    for ref, part in ((own_ref, out[:half]), (other_ref, out[half:])):
        if direct:
            tiles, xb = ref.shape[1:3]
            flat = ref.reshape(half * tiles * xb, 128)
            for t in range(tiles):
                flat[pl.ds(t * xb + pl.program_id(1), half, stride=tiles * xb), :] = part[
                    :, t * 128:(t + 1) * 128]
        else:
            ref[0] = part


def mix_kernel(got_ref, forward_high, forward_low, back_high, back_low, w_ref, out_ref,
               s_real, s_imag, m_high, m_low):
    o = pl.program_id(0)
    blocks, _, tiles, rows, _ = got_ref.shape
    channels, held, mx = s_real.shape
    modes = w_ref.shape[3]

    @pl.when(o == 0)
    def _():
        got = jnp.concatenate(
            [jnp.concatenate([got_ref[:, s, t].reshape(blocks * rows, 128) for t in range(tiles)], 1)
             for s in range(2)], 0)
        high, low = split(got)
        spectrum = dot_tn(high, forward_high[...]) + (
            dot_tn(low, forward_high[...]) + dot_tn(high, forward_low[...]))
        for i in range(channels):
            s_real[i] = spectrum[i * held:(i + 1) * held, :mx]
            s_imag[i] = spectrum[i * held:(i + 1) * held, 128:128 + mx]
        m_high[...] = jnp.zeros_like(m_high)
        m_low[...] = jnp.zeros_like(m_low)

    real = jnp.zeros((modes, mx), F32)
    imag = jnp.zeros((modes, mx), F32)
    for i in range(channels):
        w_real = w_ref[0, i, 0].astype(F32)
        w_imag = w_ref[1, i, 0].astype(F32)
        in_real = s_real[i, :modes]
        in_imag = s_imag[i, :modes]
        real += w_real * in_real - w_imag * in_imag
        imag += w_real * in_imag + w_imag * in_real
    at_row = pl.ds(pl.multiple_of(o * held, held), modes)
    for at, values in ((0, real), (128, imag)):
        high, low = split(values)
        m_high[at_row, at:at + mx] = high
        m_low[at_row, at:at + mx] = low

    @pl.when(o == pl.num_programs(0) - 1)
    def _():
        high = m_high[...]
        low = m_low[...]
        back = dot_nt(back_high[...], high) + (
            dot_nt(back_high[...], low) + dot_nt(back_low[...], high))
        for s in range(2):
            for t in range(tiles):
                out_ref[:, s, t] = back[
                    s * blocks * rows:(s + 1) * blocks * rows, t * 128:(t + 1) * 128
                ].reshape(blocks, rows, 128)


def inverse_kernel(direct, my, own_ref, other_ref, field_ref, z_ref, t_ref, pw_ref, bias_ref,
                   out_ref, v_high, v_low, local):
    channels, _, ny, nz = field_ref.shape
    group = 16
    for g in range(0, ny, 2 * group):
        pair = [field_ref[:, 0, g + k * group:g + (k + 1) * group, :].reshape(channels * group, nz)
                for k in range(2)]
        both = dot(pw_ref[...], jnp.concatenate(pair, 1))
        for k in range(2):
            local[:, g + k * group:g + (k + 1) * group, :] = both[:, k * nz:(k + 1) * nz].reshape(
                channels, group, nz)
    parts = []
    for ref in (own_ref, other_ref):
        if direct:
            half, tiles, xb, _ = ref.shape
            flat = ref.reshape(half * tiles * xb, 128)
            parts.append(jnp.concatenate(
                [flat[pl.ds(t * xb + pl.program_id(1), half, stride=tiles * xb), :]
                 for t in range(tiles)], 1))
        else:
            parts.append(ref[0])
    high, low = split(jnp.concatenate(parts, 0))
    v = dot_tn(jnp.concatenate([high, low, high], 0), z_ref[...])
    high, low = split(v)
    v_high[...] = high
    v_low[...] = low
    taps = 2 * my
    for c in range(channels):
        rows = slice(c * my, (c + 1) * my)
        top = [v_high[rows, q * nz:(q + 1) * nz] for q in range(2)]
        rest = [v_low[rows, q * nz:(q + 1) * nz] for q in range(2)]
        total = dot(t_ref[:, :2 * taps], jnp.concatenate(top + top, 0)) + dot(
            t_ref[:, :taps], jnp.concatenate(rest, 0))
        total = total + local[c] + bias_ref[c]
        out_ref[c, 0] = jax.nn.gelu(total).astype(BF16)


def whole_spec(shape):
    return pl.BlockSpec(shape, lambda *_: (0,) * len(shape))


def per_device(sizes, field, spectral_weight, pointwise_weight, bias):
    mx, my, mz = sizes
    samples, channels, x_local, y_local, nz = field.shape
    npx, npy = lax.axis_size("px"), lax.axis_size("py")
    assert samples == 1 and npy == 2
    nx, ny = x_local * npx, y_local * npy
    py = lax.axis_index("py")
    modes = spectral_weight.shape[3]
    per_kz = my // modes
    lanes_all = -(-channels * my // 128) * 128
    held = -(-modes // 16) * 16
    half = mz // npy * 2
    tiles = -(-channels * held // 128)
    direct = x_local % 8 == 0 and per_kz == 1
    halves = np.array([[0, 1], [1, 0]])

    y_angle = angles(kept(ny, my), np.arange(ny), ny)
    t_forward, t_back, z_forward, z_back = [], [], [], []
    z_angle = angles(np.arange(mz), np.arange(nz), nz)
    cosine, sine = np.cos(z_angle), np.sin(z_angle)
    weighting = (np.where(np.arange(mz) == 0, 1.0, 2.0) / (nx * ny * nz))[:, None, None]
    z_rows = np.stack([np.concatenate([cosine, -sine], 1), np.concatenate([-sine, -cosine], 1)], 1)
    z_inv = np.stack([np.concatenate([cosine, sine], 1), np.concatenate([-sine, cosine], 1)], 1) * weighting
    for p in range(npy):
        own = y_angle[:, p * y_local:(p + 1) * y_local]
        high, low = split_np(np.concatenate([np.cos(own), np.sin(own)], 0))
        t_forward.append(np.concatenate([high, low], 1))
        high, low = split_np(np.concatenate([np.cos(own), -np.sin(own)], 0).T)
        t_back.append(np.concatenate([high, low], 1))
        order = halves[p]
        rows = z_rows.reshape(npy, half, 2 * nz)[order].reshape(2 * half, 2 * nz)
        z_forward.append(np.concatenate(split_np(rows), 0))
        rows = z_inv.reshape(npy, half, 2 * nz)[order].reshape(2 * half, 2 * nz)
        high, low = split_np(rows)
        z_back.append(np.concatenate([high, high, low], 0))
    t_forward, t_back, z_forward, z_back = [
        lax.dynamic_index_in_dim(jnp.asarray(np.stack(table)), py, 0, keepdims=False)
        for table in (t_forward, t_back, z_forward, z_back)]

    x_angle = angles(kept(nx, mx), np.arange(nx), nx).T
    cosine, sine = np.cos(x_angle), np.sin(x_angle)
    x_forward = np.zeros((2, nx, 256))
    x_forward[0, :, :mx], x_forward[0, :, 128:128 + mx] = cosine, -sine
    x_forward[1, :, :mx], x_forward[1, :, 128:128 + mx] = sine, cosine
    x_back = np.zeros((2, nx, 256))
    x_back[0, :, :mx], x_back[0, :, 128:128 + mx] = cosine, -sine
    x_back[1, :, :mx], x_back[1, :, 128:128 + mx] = sine, cosine
    x_forward = [jnp.asarray(t.reshape(2 * nx, 256)) for t in split_np(x_forward)]
    x_back = [jnp.asarray(t.reshape(2 * nx, 256)) for t in split_np(x_back)]

    cells = field[0]
    xb = 8 if direct else 1
    grid = (x_local // xb, xb)
    field_spec = pl.BlockSpec((channels, 1, y_local, nz), lambda a, b: (0, a * xb + b, 0, 0))
    if direct:
        wide_shape = (half, tiles, x_local, 128)
        wide_spec = pl.BlockSpec((half, tiles, xb, 128), lambda a, b: (0, 0, a, 0))
    else:
        wide_shape = (x_local, half, lanes_all)
        wide_spec = pl.BlockSpec((1, half, lanes_all), lambda a, b: (a, 0, 0))
    limit = 60 * 2**20
    params = pltpu.CompilerParams(
        dimension_semantics=("arbitrary", "arbitrary"), vmem_limit_bytes=limit)
    own, other = pl.pallas_call(
        functools.partial(forward_kernel, direct, my),
        name="forward_yz",
        out_shape=[jax.ShapeDtypeStruct(wide_shape, F32)] * 2,
        grid=grid,
        in_specs=[field_spec, whole_spec(t_forward.shape), whole_spec(z_forward.shape)],
        out_specs=[wide_spec, wide_spec],
        scratch_shapes=[pltpu.VMEM((lanes_all, 2 * nz), BF16)] * 2,
        compiler_params=params,
    )(cells, t_forward, z_forward)

    swap = [(0, 1), (1, 0)]
    summed = own + lax.ppermute(other, "py", swap)
    if direct:
        got = lax.all_to_all(
            summed.reshape(npx, 2, tiles, x_local, 128), "px", split_axis=0, concat_axis=0, tiled=True)
    else:
        send = summed[:, :, :channels * my].reshape(
            x_local, half // 2, 2, channels, per_kz, modes).transpose(1, 4, 2, 0, 3, 5)
        got = lax.all_to_all(
            send.reshape(npx, 2, x_local, channels * modes), "px", split_axis=0, concat_axis=0,
            tiled=True)
        got = got.transpose(1, 0, 2, 3).reshape(2, nx, channels, modes)
        got = jnp.pad(got, ((0, 0), (0, 0), (0, 0), (0, held - modes)))
        got = jnp.pad(
            got.reshape(2, nx, channels * held),
            ((0, 0), (0, 0), (0, tiles * 128 - channels * held)))
        got = got.reshape(1, 2, nx, tiles, 128).transpose(0, 1, 3, 2, 4)
    mixed = pl.pallas_call(
        mix_kernel,
        name="mix_x",
        out_shape=jax.ShapeDtypeStruct(got.shape, F32),
        grid=(channels,),
        in_specs=[whole_spec(got.shape)] + [whole_spec((2 * nx, 256))] * 4 + [
            pl.BlockSpec((2, channels, 1, modes, mx), lambda o: (0, 0, o, 0, 0))],
        out_specs=whole_spec(got.shape),
        scratch_shapes=[pltpu.VMEM((channels, held, mx), F32)] * 2
        + [pltpu.VMEM((tiles * 128, 256), BF16)] * 2,
        compiler_params=pltpu.CompilerParams(
            dimension_semantics=("arbitrary",), vmem_limit_bytes=limit),
    )(got, *x_forward, *x_back, spectral_weight)
    if direct:
        back = lax.all_to_all(mixed, "px", split_axis=0, concat_axis=0, tiled=True)
        back = back.reshape(half, tiles, x_local, 128)
    else:
        mixed = mixed.transpose(0, 1, 3, 2, 4).reshape(2, npx, x_local, tiles * 128)
        mixed = mixed[..., :channels * held].reshape(2, npx, x_local, channels, held)[..., :modes]
        back = lax.all_to_all(
            mixed.transpose(1, 0, 2, 3, 4), "px", split_axis=0, concat_axis=0, tiled=True)
        back = back.reshape(half // 2, per_kz, 2, x_local, channels, modes).transpose(
            3, 0, 2, 4, 1, 5).reshape(x_local, half, channels * my)
        back = jnp.pad(back, ((0, 0), (0, 0), (0, lanes_all - channels * my)))
    partner = lax.ppermute(back, "py", swap)
    kron = jnp.kron(pointwise_weight.T.astype(F32), jnp.eye(16, dtype=F32)).astype(BF16)
    out = pl.pallas_call(
        functools.partial(inverse_kernel, direct, my),
        name="inverse_zy",
        out_shape=jax.ShapeDtypeStruct(cells.shape, BF16),
        grid=grid,
        in_specs=[wide_spec, wide_spec, field_spec, whole_spec(z_back.shape),
                  whole_spec(t_back.shape), whole_spec(kron.shape),
                  pl.BlockSpec(memory_space=pltpu.SMEM)],
        out_specs=field_spec,
        scratch_shapes=[pltpu.VMEM((lanes_all, 2 * nz), BF16)] * 2
        + [pltpu.VMEM((channels, y_local, nz), F32)],
        compiler_params=params,
    )(back, partner, cells, z_back, t_back, kron, bias)
    return out[None]


def solution(mesh):
    def per_part(field, spectral_weight, pointwise_weight, bias):
        rows, mx = spectral_weight.shape[3] * mesh.shape["px"] * mesh.shape["py"], spectral_weight.shape[4]
        mz = field.shape[4] // 4
        return per_device((mx, rows // mz, mz), field, spectral_weight, pointwise_weight, bias)

    in_specs = (
        P("groups", None, "px", "py", None),
        P(None, None, None, ("py", "px"), None),
        P(),
        P(),
    )
    out_specs = P("groups", None, "px", "py", None)
    return jax.shard_map(
        per_part, mesh=mesh, in_specs=in_specs, out_specs=out_specs, check_vma=False
    )
```

time: 640 us -> 254 us (0.40)
  local copies, waits for them, and re-layouts: 255 us -> 7.72 us
  matrix products: 150 us -> 0 us
  Pallas kernels: 0 us -> 79.9 us
  blocking collectives: 81.5 us -> 155 us
  waiting for transfers between devices: 67.5 us -> 5.5 us
  other arithmetic: 47 us -> 4.49 us
  starting transfers between devices: 18.1 us -> 0.47 us
  between operations: 14.1 us -> 0.04 us
    dot_general x7 -> x0, matrix products: 150 us -> none  [the longest x1 42.4 us: per_device(): jnp.einsum('bcxsky,skz->bcxyz', z_ready, z_inverse, precision=PRECISION_H...]
    unnamed x31 -> x8, local copies, waits for them, and re-layouts: 109 us -> 0.01 us
    pallas_call x0 -> x3, Pallas kernels: none -> 79.9 us  [the longest x1 34.9 us: per_device(): pl.pallas_call(functools.partial(inverse_kernel, direct, my), name='inver...]
    all_to_all x1 -> x2, blocking collectives: 81.5 us -> 155 us  [the longest x1 79.7 us: per_device(): lax.all_to_all(summed.reshape(npx, 2, tiles, x_local, 128), 'px', split_a...]
    all_to_all x2 -> x0, waiting for transfers between devices: 67.5 us -> none  [the longest x1 54.9 us: per_device(): lax.all_to_all(flat_modes, 'px', split_axis=4, concat_axis=2, tiled=True)]
    all_to_all x4 -> x0, local copies, waits for them, and re-layouts: 58.4 us -> none  [the longest x1 27.4 us: per_device(): lax.all_to_all(z_hat, 'py', split_axis=4, concat_axis=5, tiled=True)]
    another operation x2 -> x0, local copies, waits for them, and re-layouts: 41.4 us -> none  [the longest x1 22 us: per_device(): field[0].reshape(channels, -1)]
    transpose x2 -> x0, local copies, waits for them, and re-layouts: 26.9 us -> none  [the longest x1 20.1 us: per_device(): jnp.einsum('bcxyz,skz->bcxsky', field.astype(jnp.float32), z_forward, pre...]
  transfers between devices with their start and end apart: 3 -> 2, of which waited for: 2 -> 1; matrix products, arithmetic and copies ran while one was open for 9% -> 3% of each run, Pallas kernels for 0% -> 0%
where the time goes in v1:
time: 254 us; the launch traced here: 253 us
  blocking collectives  155 us (61%)
  Pallas kernels  79.9 us (31%)
  local copies, waits for them, and re-layouts  7.72 us (3%)
  waiting for transfers between devices  5.5 us (2%)
  other arithmetic  4.49 us (2%)
    all_to_all x1, blocking collectives, per_device(): lax.all_to_all(summed.reshape(npx, 2, tiles, x_local, 128), 'px', split_a...  79.7 us
    all_to_all x1, blocking collectives, per_device(): back = lax.all_to_all(mixed, 'px', split_axis=0, concat_axis=0, tiled=True)  74.8 us
    pallas_call x1, Pallas kernels, per_device(): pl.pallas_call(functools.partial(inverse_kernel, direct, my), name='inver...  34.9 us
    pallas_call x1, Pallas kernels, per_device(): pl.pallas_call(functools.partial(forward_kernel, direct, my), name='forwa...  25.8 us
    pallas_call x1, Pallas kernels, per_device(): pl.pallas_call(mix_kernel, name='mix_x', out_shape=jax.ShapeDtypeStruct(g...  19.2 us
    ppermute x1, waiting for transfers between devices, per_device(): summed = own + lax.ppermute(other, 'py', swap)  5.5 us
  transfers between devices with their start and end apart: 2, of which 1 were waited for; matrix products, arithmetic and copies ran while one was open for 3% of the time, Pallas kernels for 0%

profile of v1, /device:TPU:0, one launch (start us, length us, event | category | flops | bytes accessed | tf_op | source)
XLA Modules:
  0.0 252.7 jit_solution(7881671766421172558)
XLA Ops:
  0.0 1.4 dynamic-slice_bitcast_fusion.3.t_ref
  1.4 1.5 dynamic-slice_bitcast_fusion.1.z_ref
  2.9 25.8 %forward_yz.1 = (f32[32,8,24,128]{3,2,1,0:T(8,128)}, f32[32,8,24,128]{3,2,1,0:T(8,128)}) custom-call(bf16[20,24,96,128]{3,2,1,0:T(8,128)(2,1)} %bitcast.14, bf16[96,192]{1,0:T(8,128)(2,1)} %dynamic-slice_bitcast_fusion.3.t_ref, bf16[128,256]{1,0:T(8,128)(2,1)} %dynamic-slice_bitcast_fusion.1.z_ref), custom_call_target="tpu_custom_call" | custom-call | tf_op jit(solution)/shard_map/forward_yz/pallas_call | solution.py:234
  28.7 0.5 collective-permute-start
  29.2 5.5 %collective-permute-done = f32[32,8,24,128]{3,2,1,0:T(8,128)S(1)} collective-permute-done((f32[32,8,24,128]{3,2,1,0:T(8,128)}, f32[32,8,24,128]{3,2,1,0:T(8,128)S(1)}, u32[]{:S(2)}, u32[]{:S(2)}) %collective-permute-start) | collective-permute-done | bytes 3145760 | tf_op jit(solution)/shard_map/ppermute | solution.py:246
  34.7 2.4 add.13
  37.1 79.7 %all_to_all.10.got_ref = f32[16,2,8,24,128]{4,3,2,1,0:T(8,128)} all-to-all(f32[16,2,8,24,128]{4,3,2,1,0:T(8,128)S(1)} %bitcast.16), channel_id=1, replica_groups=mesh['groups'=1,'px'=16,'py'=2] {'px'}, dimensions={0} | all-to-all | bytes 6291456 | tf_op jit(solution)/shard_map/all_to_all | solution.py:248
  116.8 19.2 %mix_x.1 = f32[16,2,8,24,128]{4,3,2,1,0:T(8,128)} custom-call(f32[16,2,8,24,128]{4,3,2,1,0:T(8,128)} %all_to_all.10.got_ref, bf16[768,256]{1,0:T(8,128)(2,1)} %constant.36.clone.forward_high.back_high, bf16[768,256]{1,0:T(8,128)(2,1)} %constant.37.clone.forward_low.back_low, bf16[768,256]{1,0:T(8,128)(2,1)} %constant.36.clone.forward_high.back_high, ...), custom_call_target="tpu_custom_call" | custom-call | tf_op jit(solution)/shard_map/mix_x/pallas_call | solution.py:262
  136.0 0.0 copy-start.3
  136.0 74.8 %all_to_all.11 = f32[16,2,8,24,128]{4,3,2,1,0:T(8,128)S(1)} all-to-all(f32[16,2,8,24,128]{4,3,2,1,0:T(8,128)} %mix_x.1), channel_id=1, replica_groups=mesh['groups'=1,'px'=16,'py'=2] {'px'}, dimensions={0} | all-to-all | bytes 6291456 | tf_op jit(solution)/shard_map/all_to_all | solution.py:276
  210.8 0.0 copy-start
  210.8 0.0 copy-start.2
  210.8 0.0 copy-start.1
  210.8 0.0 collective-permute-start.1
  210.8 0.0 copy-done.3
  210.9 0.1 copy.14
  211.0 2.1 multiply_convert_fusion
  213.0 3.5 %convert_element_type.22.pw_ref = bf16[320,320]{1,0:T(8,128)(2,1)} reshape(bf16[20,16,20,16]{3,2,1,0:T(8,128)(2,1)} %multiply_convert_fusion) | data formatting | bytes 409600 | tf_op jit(solution)/shard_map/convert_element_type | solution.py:287
  216.5 0.0 copy-done.2
  216.5 0.6 dynamic-slice_bitcast_fusion.2.t_ref
  217.1 0.0 copy-done.1
  217.1 0.6 dynamic-slice_bitcast_fusion.z_ref
  217.8 0.0 collective-permute-done.1.other_ref
  217.8 0.0 copy-done
  217.8 34.9 %inverse_zy.1 = bf16[20,24,96,128]{3,2,1,0:T(8,128)(2,1)} custom-call(f32[32,8,24,128]{3,2,1,0:T(8,128)} %bitcast.18, f32[32,8,24,128]{3,2,1,0:T(8,128)} %collective-permute-done.1.other_ref, bf16[20,24,96,128]{3,2,1,0:T(8,128)(2,1)} %bitcast.15, bf16[192,256]{1,0:T(8,128)(2,1)} %dynamic-slice_bitcast_fusion.z_ref, ...), custom_call_target="tpu_custom_call" | custom-call | tf_op jit(solution)/shard_map/inverse_zy/pallas_call | solution.py:288
  (2 shorter events, 0.0 us)
Async XLA Ops:
  28.7 6.0 %collective-permute-start = (f32[32,8,24,128]{3,2,1,0:T(8,128)}, f32[32,8,24,128]{3,2,1,0:T(8,128)S(1)}, u32[]{:S(2)}, u32[]{:S(2)}) collective-permute-start(f32[32,8,24,128]{3,2,1,0:T(8,128)} %get-tuple-element.8), channel_id=1, source_target_pairs={{0,1},{1,0},{2,3},{3,2},{4,5},{5,4},{6,7},{7,6},{8,9},{9,8},{10,11... | collective-permute-start | bytes 9437192 | tf_op jit(solution)/shard_map/ppermute | solution.py:246
  136.0 74.8 %copy-start.3 = (bf16[20,20]{1,0:T(8,128)(2,1)S(1)}, bf16[20,20]{1,0:T(8,128)(2,1)}, u32[]{:S(2)}) copy-start(bf16[20,20]{1,0:T(8,128)(2,1)} %param.14) | copy-start | bytes 2404
  210.8 6.9 %copy-start = (f32[16,2,8,24,128]{4,3,2,1,0:T(8,128)}, f32[16,2,8,24,128]{4,3,2,1,0:T(8,128)S(1)}, u32[]{:S(2)}) copy-start(f32[16,2,8,24,128]{4,3,2,1,0:T(8,128)S(1)} %all_to_all.11) | copy-start | bytes 9437188
  210.8 5.7 %copy-start.2 = (bf16[2,96,192]{2,1,0:T(8,128)(2,1)S(1)}, bf16[2,96,192]{2,1,0:T(8,128)(2,1)}, u32[]{:S(2)}) copy-start(bf16[2,96,192]{2,1,0:T(8,128)(2,1)} %constant.33.clone) | copy-start | bytes 221188
  210.8 6.3 %copy-start.1 = (bf16[2,192,256]{2,1,0:T(8,128)(2,1)S(1)}, bf16[2,192,256]{2,1,0:T(8,128)(2,1)}, u32[]{:S(2)}) copy-start(bf16[2,192,256]{2,1,0:T(8,128)(2,1)} %constant.35.clone) | copy-start | bytes 589828
  210.8 6.9 %collective-permute-start.1 = (f32[32,8,24,128]{3,2,1,0:T(8,128)S(1)}, f32[32,8,24,128]{3,2,1,0:T(8,128)}, u32[]{:S(2)}, u32[]{:S(2)}) collective-permute-start(f32[32,8,24,128]{3,2,1,0:T(8,128)S(1)} %bitcast.17), channel_id=1, source_target_pairs={{0,1},{1,0},{2,3},{3,2},{4,5},{5,4},{6,7},{7,6},{8,9},{9,8},{10,11... | collective-permute-start | bytes 9437192 | tf_op jit(solution)/shard_map/ppermute | solution.py:286

commit v2 on v1

v2 whole, which is shorter than its diff:
```python
import functools

import jax
import jax.numpy as jnp
import numpy as np
from jax import lax
from jax.experimental import pallas as pl
from jax.experimental.pallas import tpu as pltpu
from jax.sharding import PartitionSpec as P


BF16 = jnp.bfloat16
F32 = jnp.float32


def kept(length, retained):
    index = np.arange(retained)
    return np.where(index < retained // 2, index, length - retained + index)


def angles(frequency, positions, length):
    return 2 * np.pi * (np.outer(frequency, positions) % length) / length


def split_np(table):
    high = table.astype(np.float32).astype(BF16)
    low = (table - high.astype(np.float64)).astype(np.float32).astype(BF16)
    return high, low


def split(values):
    high = values.astype(BF16)
    return high, (values - high.astype(F32)).astype(BF16)


def dot(a, b):
    return jnp.dot(a, b, preferred_element_type=F32)


def dot_nt(a, b):
    return lax.dot_general(a, b, (((1,), (1,)), ((), ())), preferred_element_type=F32)


def dot_tn(a, b):
    return lax.dot_general(a, b, (((0,), (0,)), ((), ())), preferred_element_type=F32)


def forward_kernel(direct, my, units, *refs):
    fields, (t_ref, z_ref, own_ref, other_ref, g_high, g_low) = refs[:units], refs[units:]
    per_unit, _, _, nz = fields[0].shape
    table = t_ref[...]
    for c in range(units * per_unit):
        cells = fields[c // per_unit][c % per_unit, 0]
        high, low = split(dot(table, jnp.concatenate([cells, cells], 0)))
        rows = slice(c * my, (c + 1) * my)
        for q in range(2):
            g_high[rows, q * nz:(q + 1) * nz] = high[q * my:(q + 1) * my]
            g_low[rows, q * nz:(q + 1) * nz] = low[q * my:(q + 1) * my]
    modes = z_ref.shape[0] // 2
    first = dot_nt(z_ref[...], g_high[...])
    out = first[:modes] + first[modes:] + dot_nt(z_ref[:modes], g_low[...])
    out = jnp.concatenate([out[:modes // 2], out[modes // 2:]], 1)
    half = modes // 4
    for ref, part in ((own_ref, out[:half]), (other_ref, out[half:])):
        if direct:
            tiles, xb = ref.shape[1:3]
            flat = ref.reshape(half * tiles * xb, 128)
            for t in range(tiles):
                flat[pl.ds(t * xb + pl.program_id(1), half, stride=tiles * xb), :] = part[
                    :, t * 128:(t + 1) * 128]
        else:
            ref[0] = part


def mix_kernel(units, has_before, last, *refs):
    got_ref, forward_high, forward_low = refs[:3]
    weights, refs = refs[3:3 + units], refs[3 + units:]
    if has_before:
        before_ref, refs = refs[0], refs[1:]
    if last:
        back_high, back_low, out_ref, s_real, s_imag, m_high, m_low = refs
    else:
        out_ref, s_real, s_imag = refs
    o = pl.program_id(0)
    blocks, tiles, rows, _ = got_ref.shape
    channels, held, mx = s_real.shape
    per_unit = channels // units
    modes = weights[0].shape[3]
    lanes = channels * held

    @pl.when(o == 0)
    def _():
        got = jnp.concatenate(
            [got_ref[:, t].reshape(blocks * rows, 128) for t in range(tiles)], 1)
        high, low = split(jnp.concatenate([got[:, :lanes], got[:, lanes:2 * lanes]], 0))
        spectrum = dot_tn(high, forward_high[...]) + (
            dot_tn(low, forward_high[...]) + dot_tn(high, forward_low[...]))
        for i in range(channels):
            s_real[i] = spectrum[i * held:(i + 1) * held, :mx]
            s_imag[i] = spectrum[i * held:(i + 1) * held, 128:128 + mx]
        if last:
            m_high[...] = jnp.zeros_like(m_high)
            m_low[...] = jnp.zeros_like(m_low)

    if has_before:
        real, imag = before_ref[0, 0], before_ref[0, 1]
    else:
        real, imag = jnp.zeros((modes, mx), F32), jnp.zeros((modes, mx), F32)
    for i in range(channels):
        w_real = weights[i // per_unit][0, i % per_unit, 0].astype(F32)
        w_imag = weights[i // per_unit][1, i % per_unit, 0].astype(F32)
        in_real = s_real[i, :modes]
        in_imag = s_imag[i, :modes]
        real += w_real * in_real - w_imag * in_imag
        imag += w_real * in_imag + w_imag * in_real
    if not last:
        out_ref[0, 0] = real
        out_ref[0, 1] = imag
        return
    at_row = pl.ds(pl.multiple_of(o * held, held), modes)
    for at, values in ((0, real), (128, imag)):
        high, low = split(values)
        m_high[at_row, at:at + mx] = high
        m_low[at_row, at:at + mx] = low

    @pl.when(o == pl.num_programs(0) - 1)
    def _():
        high = m_high[...]
        low = m_low[...]
        back = dot_nt(back_high[...], high) + (
            dot_nt(back_high[...], low) + dot_nt(back_low[...], high))
        back = jnp.concatenate([back[:blocks * rows], back[blocks * rows:]], 1)
        for t in range(out_ref.shape[1]):
            out_ref[:, t] = back[:, t * 128:(t + 1) * 128].reshape(blocks, rows, 128)


def inverse_kernel(direct, my, start, chained, *refs):
    (own_ref, other_ref, field_ref, z_ref, t_ref, pw_ref, bias_ref) = refs[:7]
    out_ref, v_high, v_low, local = refs[7 + chained:]
    channels, _, ny, nz = field_ref.shape
    outs = out_ref.shape[0]
    group = 16
    for g in range(0, ny, 2 * group):
        pair = [field_ref[:, 0, g + k * group:g + (k + 1) * group, :].reshape(channels * group, nz)
                for k in range(2)]
        both = dot(pw_ref[...], jnp.concatenate(pair, 1))
        for k in range(2):
            local[:, g + k * group:g + (k + 1) * group, :] = both[:, k * nz:(k + 1) * nz].reshape(
                outs, group, nz)
    parts = []
    for ref in (own_ref, other_ref):
        if direct:
            half, tiles, xb, _ = ref.shape
            flat = ref.reshape(half * tiles * xb, 128)
            parts.append(jnp.concatenate(
                [flat[pl.ds(t * xb + pl.program_id(1), half, stride=tiles * xb), :]
                 for t in range(tiles)], 1))
        else:
            parts.append(ref[0])
    wide = jnp.concatenate(parts, 0)
    lanes = outs * my
    high, low = split(jnp.concatenate([wide[:, :lanes], wide[:, lanes:2 * lanes]], 0))
    high, low = split(dot_tn(jnp.concatenate([high, low, high], 0), z_ref[...]))
    v_high[...] = high
    v_low[...] = low
    taps = 2 * my
    for c in range(outs):
        rows = slice(c * my, (c + 1) * my)
        top = [v_high[rows, q * nz:(q + 1) * nz] for q in range(2)]
        rest = [v_low[rows, q * nz:(q + 1) * nz] for q in range(2)]
        total = dot(t_ref[:, :2 * taps], jnp.concatenate(top + top, 0)) + dot(
            t_ref[:, :taps], jnp.concatenate(rest, 0))
        total = total + local[c] + bias_ref[start + c]
        out_ref[c, 0] = jax.nn.gelu(total).astype(BF16)


def whole_spec(shape):
    return pl.BlockSpec(shape, lambda *_: (0,) * len(shape))


def per_device(sizes, field, spectral_weight, pointwise_weight, bias):
    mx, my, mz = sizes
    samples, channels, x_local, y_local, nz = field.shape
    npx, npy = lax.axis_size("px"), lax.axis_size("py")
    assert samples == 1 and npy == 2
    nx, ny = x_local * npx, y_local * npy
    py = lax.axis_index("py")
    modes = spectral_weight.shape[3]
    per_kz = my // modes
    held = -(-modes // 16) * 16
    half = mz // npy
    per_unit = 4 if channels % 4 == 0 else channels
    direct = x_local % 8 == 0 and per_kz == 1 and 2 * per_unit * my % 128 == 0
    every = list(range(channels // per_unit))
    halves = np.array([[0, 1], [1, 0]])

    y_angle = angles(kept(ny, my), np.arange(ny), ny)
    t_forward, t_back, z_forward, z_back = [], [], [], []
    z_angle = angles(np.arange(mz), np.arange(nz), nz)
    cosine, sine = np.cos(z_angle), np.sin(z_angle)
    weighting = (np.where(np.arange(mz) == 0, 1.0, 2.0) / (nx * ny * nz))[:, None]
    z_rows = np.stack([np.concatenate([cosine, -sine], 1), np.concatenate([-sine, -cosine], 1)], 0)
    z_inv = np.stack([np.concatenate([cosine, sine], 1), np.concatenate([-sine, cosine], 1)], 0) * weighting
    for p in range(npy):
        own = y_angle[:, p * y_local:(p + 1) * y_local]
        high, low = split_np(np.concatenate([np.cos(own), np.sin(own)], 0))
        t_forward.append(np.concatenate([high, low], 1))
        high, low = split_np(np.concatenate([np.cos(own), -np.sin(own)], 0).T)
        t_back.append(np.concatenate([high, low], 1))
        order = halves[p]
        rows = z_rows.reshape(2, npy, half, 2 * nz)[:, order].reshape(2 * mz, 2 * nz)
        z_forward.append(np.concatenate(split_np(rows), 0))
        rows = z_inv.reshape(2, npy, half, 2 * nz)[:, order].reshape(2 * mz, 2 * nz)
        high, low = split_np(rows)
        z_back.append(np.concatenate([high, high, low], 0))
    t_forward, t_back, z_forward, z_back = [
        lax.dynamic_index_in_dim(jnp.asarray(np.stack(table)), py, 0, keepdims=False)
        for table in (t_forward, t_back, z_forward, z_back)]

    x_angle = angles(kept(nx, mx), np.arange(nx), nx).T
    cosine, sine = np.cos(x_angle), np.sin(x_angle)
    x_forward = np.zeros((2, nx, 256))
    x_forward[0, :, :mx], x_forward[0, :, 128:128 + mx] = cosine, -sine
    x_forward[1, :, :mx], x_forward[1, :, 128:128 + mx] = sine, cosine
    x_back = np.zeros((2, nx, 256))
    x_back[0, :, :mx], x_back[0, :, 128:128 + mx] = cosine, -sine
    x_back[1, :, :mx], x_back[1, :, 128:128 + mx] = sine, cosine
    x_forward = [jnp.asarray(t.reshape(2 * nx, 256)) for t in split_np(x_forward)]
    x_back = [jnp.asarray(t.reshape(2 * nx, 256)) for t in split_np(x_back)]

    cells = field[0]
    xb = 8 if direct else 1
    grid = (x_local // xb, xb)
    limit = 60 * 2**20
    params = pltpu.CompilerParams(
        dimension_semantics=("arbitrary", "arbitrary"), vmem_limit_bytes=limit)
    swap = [(0, 1), (1, 0)]

    def field_spec(size, at):
        return pl.BlockSpec((size, 1, y_local, nz), lambda a, b: (at, a * xb + b, 0, 0))

    def wide_of(count):
        lanes = 2 * count * my
        if direct:
            return (half, lanes // 128, x_local, 128), pl.BlockSpec(
                (half, lanes // 128, xb, 128), lambda a, b: (0, 0, a, 0))
        return (x_local, half, lanes), pl.BlockSpec((1, half, lanes), lambda a, b: (a, 0, 0))

    def to_modes(units):
        count = len(units) * per_unit
        shape, spec = wide_of(count)
        own, other = pl.pallas_call(
            functools.partial(forward_kernel, direct, my, len(units)),
            name="forward_yz",
            out_shape=[jax.ShapeDtypeStruct(shape, F32)] * 2,
            grid=grid,
            in_specs=[field_spec(per_unit, u) for u in units]
            + [whole_spec(t_forward.shape), whole_spec(z_forward.shape)],
            out_specs=[spec, spec],
            scratch_shapes=[pltpu.VMEM((count * my, 2 * nz), BF16)] * 2,
            compiler_params=params,
            cost_estimate=pl.CostEstimate(
                flops=count * x_local * 40_000_000, transcendentals=0,
                bytes_accessed=count * x_local * y_local * nz * 4),
        )(*[cells] * len(units), t_forward, z_forward)
        summed = own + lax.ppermute(other, "py", swap)
        if direct:
            return lax.all_to_all(summed, "px", split_axis=0, concat_axis=0, tiled=True)
        send = summed.reshape(x_local, half, 2, count, per_kz, modes).transpose(1, 4, 2, 0, 3, 5)
        got = lax.all_to_all(
            send.reshape(npx, 2, x_local, count * modes), "px", split_axis=0, concat_axis=0,
            tiled=True)
        got = got.reshape(npx, 2, x_local, count, modes).transpose(0, 2, 1, 3, 4)
        got = jnp.pad(got, ((0, 0),) * 4 + ((0, held - modes),)).reshape(nx, 2 * count * held)
        tiles = -(-got.shape[1] // 128)
        got = jnp.pad(got, ((0, 0), (0, tiles * 128 - got.shape[1])))
        return got.reshape(1, nx, tiles, 128).transpose(0, 2, 1, 3)

    def mix(got, units, before, out_units):
        count, outs = len(units) * per_unit, len(out_units) * per_unit
        first = out_units[0] * per_unit
        last = before is not None or len(units) == len(every)
        blocks, _, rows, _ = got.shape

        def weight_spec(u):
            return pl.BlockSpec((2, per_unit, 1, modes, mx), lambda o: (0, u, first + o, 0, 0))

        specs = [whole_spec(got.shape)] + [whole_spec((2 * nx, 256))] * 2
        specs += [weight_spec(u) for u in units]
        operands = [got, *x_forward] + [spectral_weight] * len(units)
        if before is not None:
            specs.append(pl.BlockSpec((1, 2, modes, mx), lambda o: (first + o, 0, 0, 0)))
            operands.append(before)
        scratch = [pltpu.VMEM((count, held, mx), F32)] * 2
        if last:
            specs += [whole_spec((2 * nx, 256))] * 2
            operands += x_back
            shape = (blocks, -(-2 * outs * held // 128), rows, 128)
            out_spec = whole_spec(shape)
            padded = outs * held if direct else shape[1] * 64
            scratch += [pltpu.VMEM((padded, 256), BF16)] * 2
        else:
            shape = (outs, 2, modes, mx)
            out_spec = pl.BlockSpec((1, 2, modes, mx), lambda o: (o, 0, 0, 0))
        return pl.pallas_call(
            functools.partial(mix_kernel, len(units), before is not None, last),
            name="mix_x",
            out_shape=jax.ShapeDtypeStruct(shape, F32),
            grid=(outs,),
            in_specs=specs,
            out_specs=out_spec,
            scratch_shapes=scratch,
            compiler_params=pltpu.CompilerParams(
                dimension_semantics=("arbitrary",), vmem_limit_bytes=limit),
            cost_estimate=pl.CostEstimate(
                flops=count * outs * 40_000_000, transcendentals=0,
                bytes_accessed=4 * count * outs * modes * 128),
        )(*operands)

    def send_back(mixed, count):
        if direct:
            return lax.all_to_all(mixed, "px", split_axis=0, concat_axis=0, tiled=True)
        tiles = mixed.shape[1]
        mixed = mixed.transpose(0, 2, 1, 3).reshape(npx, x_local, tiles * 128)
        mixed = mixed[..., :2 * count * held].reshape(npx, x_local, 2, count, held)[..., :modes]
        back = lax.all_to_all(mixed, "px", split_axis=0, concat_axis=0, tiled=True)
        return back.reshape(half, per_kz, x_local, 2, count, modes).transpose(
            2, 0, 3, 4, 1, 5).reshape(x_local, half, 2 * count * my)

    kron = jnp.kron(pointwise_weight.T.astype(F32), jnp.eye(16, dtype=F32)).astype(BF16)

    def to_cells(back, units, so_far):
        count = len(units) * per_unit
        first = units[0] * per_unit
        partner = lax.ppermute(back, "py", swap)
        _, spec = wide_of(count)
        weights = kron[first * 16:(first + count) * 16]
        operands = [back, partner, cells, z_back, t_back, weights, bias]
        specs = [spec, spec, field_spec(channels, 0), whole_spec(z_back.shape),
                 whole_spec(t_back.shape), whole_spec(weights.shape),
                 pl.BlockSpec(memory_space=pltpu.SMEM)]
        chained = so_far is not None
        if chained:
            operands.append(so_far)
            specs.append(pl.BlockSpec(memory_space=pl.ANY))
        return pl.pallas_call(
            functools.partial(inverse_kernel, direct, my, first, int(chained)),
            name="inverse_zy",
            out_shape=jax.ShapeDtypeStruct(cells.shape, BF16),
            grid=grid,
            in_specs=specs,
            out_specs=field_spec(count, first // count),
            scratch_shapes=[pltpu.VMEM((count * my, 2 * nz), BF16)] * 2
            + [pltpu.VMEM((count, y_local, nz), F32)],
            input_output_aliases={7: 0} if chained else {},
            compiler_params=params,
            cost_estimate=pl.CostEstimate(
                flops=count * x_local * 60_000_000, transcendentals=0,
                bytes_accessed=count * x_local * y_local * nz * 6),
        )(*operands)

    if direct and len(every) == 5:
        in_chunks, out_chunks = [every[:2], every[2:]], [every[:2], every[2:4], every[4:]]
    else:
        in_chunks, out_chunks = [every], [every]
    before = None
    for units in in_chunks[:-1]:
        before = mix(to_modes(units), units, before, every)
    got = to_modes(in_chunks[-1])
    returned = []
    for units in out_chunks:
        mixed = mix(got, in_chunks[-1], before, units)
        returned.append(send_back(mixed, len(units) * per_unit))
    out = None
    for back, units in zip(returned, out_chunks):
        out = to_cells(back, units, out)
    return out[None]


def solution(mesh):
    def per_part(field, spectral_weight, pointwise_weight, bias):
        rows, mx = spectral_weight.shape[3] * mesh.shape["px"] * mesh.shape["py"], spectral_weight.shape[4]
        mz = field.shape[4] // 4
        return per_device((mx, rows // mz, mz), field, spectral_weight, pointwise_weight, bias)

    in_specs = (
        P("groups", None, "px", "py", None),
        P(None, None, None, ("py", "px"), None),
        P(),
        P(),
    )
    out_specs = P("groups", None, "px", "py", None)
    return jax.shard_map(
        per_part, mesh=mesh, in_specs=in_specs, out_specs=out_specs, check_vma=False
    )
```

time: 254 us -> 287 us (1.13)
  blocking collectives: 155 us -> 0 us
  waiting for transfers between devices: 5.5 us -> 76.7 us
  Pallas kernels: 79.9 us -> 151 us
  starting transfers between devices: 0.47 us -> 36.9 us
  local copies, waits for them, and re-layouts: 7.72 us -> 12.1 us
    all_to_all x2 -> x0, blocking collectives: 155 us -> none  [the longest x1 79.7 us: per_device(): lax.all_to_all(summed.reshape(npx, 2, tiles, x_local, 128), 'px', split_a...]
    pallas_call x3 -> x9, Pallas kernels: 79.9 us -> 151 us  [the longest x3 70.1 us: to_cells(): pl.pallas_call(functools.partial(inverse_kernel, direct, my, first, int(c...]
    all_to_all x0 -> x5, waiting for transfers between devices: none -> 70.1 us  [the longest x3 46 us: send_back(): return lax.all_to_all(mixed, 'px', split_axis=0, concat_axis=0, tiled=True)]
    all_to_all x0 -> x5, starting transfers between devices: none -> 36.3 us  [the longest x3 21.2 us: send_back(): return lax.all_to_all(mixed, 'px', split_axis=0, concat_axis=0, tiled=True)]
    unnamed x8 -> x18, local copies, waits for them, and re-layouts: 0.01 us -> 4.19 us
    slice x0 -> x8, local copies, waits for them, and re-layouts: none -> 3.76 us  [to_cells(): weights = kron[first * 16:(first + count) * 16]]
    convert_element_type x2 -> x0, local copies, waits for them, and re-layouts: 3.55 us -> none  [the longest x1 3.46 us: per_device(): jnp.kron(pointwise_weight.T.astype(F32), jnp.eye(16, dtype=F32))]
    add x1 -> x2, other arithmetic: 2.43 us -> 5.36 us  [to_modes(): summed = own + lax.ppermute(other, 'py', swap)]
  transfers between devices with their start and end apart: 2 -> 10, of which waited for: 1 -> 6; matrix products, arithmetic and copies ran while one was open for 3% -> 3% of each run, Pallas kernels for 0% -> 36%
where the time goes in v2:
time: 287 us; the launch traced here: 283 us
  Pallas kernels  151 us (53%)
  waiting for transfers between devices  76.7 us (27%)
  starting transfers between devices  36.9 us (13%)
  local copies, waits for them, and re-layouts  12.1 us (4%)
  other arithmetic  5.75 us (2%)
    pallas_call x3, Pallas kernels, to_cells(): pl.pallas_call(functools.partial(inverse_kernel, direct, my, first, int(c...  70.1 us
    all_to_all x3, waiting for transfers between devices, send_back(): return lax.all_to_all(mixed, 'px', split_axis=0, concat_axis=0, tiled=True)  46 us
    pallas_call x2, Pallas kernels, to_modes(): pl.pallas_call(functools.partial(forward_kernel, direct, my, len(units)),...  42.9 us
    pallas_call x4, Pallas kernels, mix(): pl.pallas_call(functools.partial(mix_kernel, len(units), before is not No...  38.2 us
    all_to_all x2, waiting for transfers between devices, to_modes(): return lax.all_to_all(summed, 'px', split_axis=0, concat_axis=0, tiled=True)  24.2 us
    all_to_all x3, starting transfers between devices, send_back(): return lax.all_to_all(mixed, 'px', split_axis=0, concat_axis=0, tiled=True)  21.2 us
    all_to_all x2, starting transfers between devices, to_modes(): return lax.all_to_all(summed, 'px', split_axis=0, concat_axis=0, tiled=True)  15.1 us
    ppermute x2, waiting for transfers between devices, to_modes(): summed = own + lax.ppermute(other, 'py', swap)  6.58 us
  transfers between devices with their start and end apart: 10, of which 6 were waited for; matrix products, arithmetic and copies ran while one was open for 3% of the time, Pallas kernels for 36%

profile of v2, /device:TPU:0, one launch (start us, length us, event | category | flops | bytes accessed | tf_op | source)
XLA Modules:
  0.0 282.9 jit_solution(12691844528213602316)
XLA Ops:
  0.0 1.4 dynamic-slice_bitcast_fusion.3.refs_3_.refs_2_
  1.4 1.5 dynamic-slice_bitcast_fusion.1.refs_4_.refs_3_
  2.9 19.9 %forward_yz.3 = (f32[16,6,24,128]{3,2,1,0:T(8,128)}, f32[16,6,24,128]{3,2,1,0:T(8,128)}) custom-call(bf16[20,24,96,128]{3,2,1,0:T(8,128)(2,1)} %bitcast.22, bf16[20,24,96,128]{3,2,1,0:T(8,128)(2,1)} %bitcast.23, bf16[96,192]{1,0:T(8,128)(2,1)} %dynamic-slice_bitcast_fusion.3.refs_3_.refs_2_, bf16[128,256]{1,0:T(8,128)(2,1)} %dynamic-slice_bitcast_fusion.1.refs_4_.refs_3_), custom_call_target="tpu_custom_call" | custom-call | flops 7680000000 | bytes 9437184 | tf_op jit(solution)/shard_map/forward_yz/pallas_call | solution.py:252
  23.3 2.7 collective-permute-done.1
  26.0 2.4 add.17
  28.4 8.2 %all-to-all-start.1 = ((f32[16,6,24,128]{3,2,1,0:T(8,128)}), f32[16,6,24,128]{3,2,1,0:T(8,128)S(1)}, u32[]{:S(2)}, u32[]{:S(2)}) async-start(f32[16,6,24,128]{3,2,1,0:T(8,128)} %add.17), calls=%async_computation.1 | async-start | bytes 2359296 | tf_op jit(solution)/shard_map/all_to_all | solution.py:268
  36.7 23.0 %forward_yz.2 = (f32[16,9,24,128]{3,2,1,0:T(8,128)}, f32[16,9,24,128]{3,2,1,0:T(8,128)}) custom-call(bf16[20,24,96,128]{3,2,1,0:T(8,128)(2,1)} %bitcast.24, bf16[20,24,96,128]{3,2,1,0:T(8,128)(2,1)} %bitcast.25, bf16[20,24,96,128]{3,2,1,0:T(8,128)(2,1)} %bitcast.26, bf16[96,192]{1,0:T(8,128)(2,1)} %dynamic-slice_bitcast_fusion.3.refs_3_.refs_2_, ...), custom_call_target="tpu_custom_call" | custom-call | flops 11520000000 | bytes 14155776 | tf_op jit(solution)/shard_map/forward_yz/pallas_call | solution.py:252
  59.6 3.9 %collective-permute-done = f32[16,9,24,128]{3,2,1,0:T(8,128)S(1)} collective-permute-done((f32[16,9,24,128]{3,2,1,0:T(8,128)}, f32[16,9,24,128]{3,2,1,0:T(8,128)S(1)}, u32[]{:S(2)}, u32[]{:S(2)}) %collective-permute-start) | collective-permute-done | bytes 1769504 | tf_op jit(solution)/shard_map/ppermute | solution.py:266
  63.5 2.9 %add.16 = f32[16,9,24,128]{3,2,1,0:T(8,128)} add(f32[16,9,24,128]{3,2,1,0:T(8,128)} %get-tuple-element.9, f32[16,9,24,128]{3,2,1,0:T(8,128)S(1)} %collective-permute-done) | non-fusion elementwise | flops 442368 | bytes 5308416 | tf_op jit(solution)/shard_map/add | solution.py:266
  66.5 1.1 copy-done.3
  67.5 6.9 %all-to-all-start = ((f32[16,9,24,128]{3,2,1,0:T(8,128)}), f32[16,9,24,128]{3,2,1,0:T(8,128)S(1)}, u32[]{:S(2)}, u32[]{:S(2)}) async-start(f32[16,9,24,128]{3,2,1,0:T(8,128)} %add.16), calls=%async_computation | async-start | bytes 3538944 | tf_op jit(solution)/shard_map/all_to_all | solution.py:268
  74.4 13.5 %mix_x.4.refs_6_ = f32[20,2,48,96]{3,2,1,0:T(8,128)} custom-call(f32[16,6,24,128]{3,2,1,0:T(8,128)} %copy-done.3, bf16[768,256]{1,0:T(8,128)(2,1)} %constant.36.clone.refs_1_.refs_7_, bf16[768,256]{1,0:T(8,128)(2,1)} %constant.37.clone.refs_2_.refs_8_, bf16[2,20,20,48,96]{4,3,2,1,0:T(8,128)(2,1)} %refs_5_.5, bf16[2,20,20,48,96]{4,3,2,1,0:T(8,128)(2,1)} %refs_5_.5), custom_call_target="tpu_custom_call" | custom-call | flops 6400000000 | bytes 3932160 | tf_op jit(solution)/shard_map/mix_x/pallas_call | solution.py:305
  87.9 24.1 %all-to-all-done.refs_0_ = f32[16,9,24,128]{3,2,1,0:T(8,128)S(1)} async-done(((f32[16,9,24,128]{3,2,1,0:T(8,128)}), f32[16,9,24,128]{3,2,1,0:T(8,128)S(1)}, u32[]{:S(2)}, u32[]{:S(2)}) %all-to-all-start) | async-done | bytes 1769504 | tf_op jit(solution)/shard_map/all_to_all | solution.py:268
  112.0 1.2 copy-done
  113.2 9.2 %mix_x.7 = f32[16,6,24,128]{3,2,1,0:T(8,128)} custom-call(f32[16,9,24,128]{3,2,1,0:T(8,128)} %copy-done, bf16[768,256]{1,0:T(8,128)(2,1)} %constant.36.clone.refs_1_.refs_7_, bf16[768,256]{1,0:T(8,128)(2,1)} %constant.37.clone.refs_2_.refs_8_, bf16[2,20,20,48,96]{4,3,2,1,0:T(8,128)(2,1)} %refs_5_.5, bf16[2,20,20,48,96]{4,3,2,1,0:T(8,128)(2,1)} %refs_5_.5, ...), custom_call_target="tpu_custom_call" | custom-call | flops 3840000000 | bytes 2359296 | tf_op jit(solution)/shard_map/mix_x/pallas_call | solution.py:305
  122.4 8.8 %all-to-all-start.4 = ((f32[16,6,24,128]{3,2,1,0:T(8,128)}), f32[16,6,24,128]{3,2,1,0:T(8,128)}, u32[]{:S(2)}, u32[]{:S(2)}) async-start(f32[16,6,24,128]{3,2,1,0:T(8,128)} %mix_x.7), calls=%async_computation.4 | async-start | bytes 2359296 | tf_op jit(solution)/shard_map/all_to_all | solution.py:322
  131.2 9.2 %mix_x.6 = f32[16,6,24,128]{3,2,1,0:T(8,128)} custom-call(f32[16,9,24,128]{3,2,1,0:T(8,128)} %copy-done, bf16[768,256]{1,0:T(8,128)(2,1)} %constant.36.clone.refs_1_.refs_7_, bf16[768,256]{1,0:T(8,128)(2,1)} %constant.37.clone.refs_2_.refs_8_, bf16[2,20,20,48,96]{4,3,2,1,0:T(8,128)(2,1)} %refs_5_.5, bf16[2,20,20,48,96]{4,3,2,1,0:T(8,128)(2,1)} %refs_5_.5, ...), custom_call_target="tpu_custom_call" | custom-call | flops 3840000000 | bytes 2359296 | tf_op jit(solution)/shard_map/mix_x/pallas_call | solution.py:305
  140.4 17.0 %all-to-all-done.4.refs_0_ = f32[16,6,24,128]{3,2,1,0:T(8,128)} async-done(((f32[16,6,24,128]{3,2,1,0:T(8,128)}), f32[16,6,24,128]{3,2,1,0:T(8,128)}, u32[]{:S(2)}, u32[]{:S(2)}) %all-to-all-start.4) | async-done | bytes 1179680 | tf_op jit(solution)/shard_map/all_to_all | solution.py:322
  157.4 6.2 %all-to-all-start.3 = ((f32[16,6,24,128]{3,2,1,0:T(8,128)}), f32[16,6,24,128]{3,2,1,0:T(8,128)S(1)}, u32[]{:S(2)}, u32[]{:S(2)}) async-start(f32[16,6,24,128]{3,2,1,0:T(8,128)} %mix_x.6), calls=%async_computation.3 | async-start | bytes 2359296 | tf_op jit(solution)/shard_map/all_to_all | solution.py:322
  163.7 6.4 %mix_x.5 = f32[16,3,24,128]{3,2,1,0:T(8,128)} custom-call(f32[16,9,24,128]{3,2,1,0:T(8,128)} %copy-done, bf16[768,256]{1,0:T(8,128)(2,1)} %constant.36.clone.refs_1_.refs_7_, bf16[768,256]{1,0:T(8,128)(2,1)} %constant.37.clone.refs_2_.refs_8_, bf16[2,20,20,48,96]{4,3,2,1,0:T(8,128)(2,1)} %refs_5_.5, bf16[2,20,20,48,96]{4,3,2,1,0:T(8,128)(2,1)} %refs_5_.5, ...), custom_call_target="tpu_custom_call" | custom-call | flops 1920000000 | bytes 1179648 | tf_op jit(solution)/shard_map/mix_x/pallas_call | solution.py:305
  170.1 19.2 %all-to-all-done.3.refs_0_ = f32[16,6,24,128]{3,2,1,0:T(8,128)S(1)} async-done(((f32[16,6,24,128]{3,2,1,0:T(8,128)}), f32[16,6,24,128]{3,2,1,0:T(8,128)S(1)}, u32[]{:S(2)}, u32[]{:S(2)}) %all-to-all-start.3) | async-done | bytes 1179680 | tf_op jit(solution)/shard_map/all_to_all | solution.py:322
  189.3 6.2 %all-to-all-start.2 = ((f32[16,3,24,128]{3,2,1,0:T(8,128)}), f32[16,3,24,128]{3,2,1,0:T(8,128)}, u32[]{:S(2)}, u32[]{:S(2)}) async-start(f32[16,3,24,128]{3,2,1,0:T(8,128)} %mix_x.5), calls=%async_computation.2 | async-start | bytes 1179648 | tf_op jit(solution)/shard_map/all_to_all | solution.py:322
  196.3 0.7 copy.18.refs_5_
  197.8 0.8 copy.16.refs_5_
  199.0 0.8 copy.17.refs_5_
  199.7 0.7 dynamic-slice_bitcast_fusion.refs_3_
  201.0 9.8 %all-to-all-done.2.refs_0_ = f32[16,3,24,128]{3,2,1,0:T(8,128)} async-done(((f32[16,3,24,128]{3,2,1,0:T(8,128)}), f32[16,3,24,128]{3,2,1,0:T(8,128)}, u32[]{:S(2)}, u32[]{:S(2)}) %all-to-all-start.2) | async-done | bytes 589856 | tf_op jit(solution)/shard_map/all_to_all | solution.py:322
  210.8 24.2 %inverse_zy.3.refs_7_ = bf16[20,24,96,128]{3,2,1,0:T(8,128)(2,1)} custom-call(f32[16,6,24,128]{3,2,1,0:T(8,128)} %all-to-all-done.4.refs_0_, f32[16,6,24,128]{3,2,1,0:T(8,128)} %collective-permute-done.4.refs_1_, bf16[20,24,96,128]{3,2,1,0:T(8,128)(2,1)} %bitcast.27, bf16[192,256]{1,0:T(8,128)(2,1)} %dynamic-slice_bitcast_fusion.refs_3_, ...), custom_call_target="tpu_custom_call" | custom-call | flops 11520000000 | bytes 14155776 | tf_op jit(solution)/shard_map/inverse_zy/pallas_call | solution.py:346
  235.1 1.0 copy-done.8
  236.1 24.2 %inverse_zy.4.refs_7_ = bf16[20,24,96,128]{3,2,1,0:T(8,128)(2,1)} custom-call(f32[16,6,24,128]{3,2,1,0:T(8,128)} %copy-done.1, f32[16,6,24,128]{3,2,1,0:T(8,128)} %copy-done.8, bf16[20,24,96,128]{3,2,1,0:T(8,128)(2,1)} %bitcast.28, bf16[192,256]{1,0:T(8,128)(2,1)} %dynamic-slice_bitcast_fusion.refs_3_, ...), custom_call_target="tpu_custom_call", output_to_operand_aliasing={{}: (7, {})} | custom-call | flops 11520000000 | bytes 14155776 | tf_op jit(solution)/shard_map/inverse_zy/pallas_call | solution.py:346
  260.3 0.8 copy-done.4
  261.2 21.7 %inverse_zy.5 = bf16[20,24,96,128]{3,2,1,0:T(8,128)(2,1)} custom-call(f32[16,3,24,128]{3,2,1,0:T(8,128)} %all-to-all-done.2.refs_0_, f32[16,3,24,128]{3,2,1,0:T(8,128)} %copy-done.4, bf16[20,24,96,128]{3,2,1,0:T(8,128)(2,1)} %bitcast.29, bf16[192,256]{1,0:T(8,128)(2,1)} %dynamic-slice_bitcast_fusion.refs_3_, ...), custom_call_target="tpu_custom_call", output_to_operand_aliasing={{}: (7, {})} | custom-call | flops 5760000000 | bytes 7077888 | tf_op jit(solution)/shard_map/inverse_zy/pallas_call | solution.py:346
  (32 shorter events, 3.2 us)
Async XLA Ops:
  22.8 3.2 %collective-permute-start.1 = (f32[16,6,24,128]{3,2,1,0:T(8,128)}, f32[16,6,24,128]{3,2,1,0:T(8,128)S(1)}, u32[]{:S(2)}, u32[]{:S(2)}) collective-permute-start(f32[16,6,24,128]{3,2,1,0:T(8,128)} %get-tuple-element.12), channel_id=1, source_target_pairs={{0,1},{1,0},{2,3},{3,2},{4,5},{5,4},{6,7},{7,6},{8,9},{9,8},{10,11... | collective-permute-start | bytes 3538952 | tf_op jit(solution)/shard_map/ppermute | solution.py:266
  28.4 38.0 %all-to-all-start.1 = ((f32[16,6,24,128]{3,2,1,0:T(8,128)}), f32[16,6,24,128]{3,2,1,0:T(8,128)S(1)}, u32[]{:S(2)}, u32[]{:S(2)}) async-start(f32[16,6,24,128]{3,2,1,0:T(8,128)} %add.17), calls=%async_computation.1 | async-start | bytes 2359296 | tf_op jit(solution)/shard_map/all_to_all | solution.py:268
  59.6 3.9 %collective-permute-start = (f32[16,9,24,128]{3,2,1,0:T(8,128)}, f32[16,9,24,128]{3,2,1,0:T(8,128)S(1)}, u32[]{:S(2)}, u32[]{:S(2)}) collective-permute-start(f32[16,9,24,128]{3,2,1,0:T(8,128)} %get-tuple-element.10), channel_id=1, source_target_pairs={{0,1},{1,0},{2,3},{3,2},{4,5},{5,4},{6,7},{7,6},{8,9},{9,8},{10,11... | collective-permute-start | bytes 5308424 | tf_op jit(solution)/shard_map/ppermute | solution.py:266
  66.5 1.1 copy-start.3
  67.5 44.5 %all-to-all-start = ((f32[16,9,24,128]{3,2,1,0:T(8,128)}), f32[16,9,24,128]{3,2,1,0:T(8,128)S(1)}, u32[]{:S(2)}, u32[]{:S(2)}) async-start(f32[16,9,24,128]{3,2,1,0:T(8,128)} %add.16), calls=%async_computation | async-start | bytes 3538944 | tf_op jit(solution)/shard_map/all_to_all | solution.py:268
  112.0 1.2 copy-start
  122.4 35.0 %all-to-all-start.4 = ((f32[16,6,24,128]{3,2,1,0:T(8,128)}), f32[16,6,24,128]{3,2,1,0:T(8,128)}, u32[]{:S(2)}, u32[]{:S(2)}) async-start(f32[16,6,24,128]{3,2,1,0:T(8,128)} %mix_x.7), calls=%async_computation.4 | async-start | bytes 2359296 | tf_op jit(solution)/shard_map/all_to_all | solution.py:322
  157.4 31.9 %all-to-all-start.3 = ((f32[16,6,24,128]{3,2,1,0:T(8,128)}), f32[16,6,24,128]{3,2,1,0:T(8,128)S(1)}, u32[]{:S(2)}, u32[]{:S(2)}) async-start(f32[16,6,24,128]{3,2,1,0:T(8,128)} %mix_x.6), calls=%async_computation.3 | async-start | bytes 2359296 | tf_op jit(solution)/shard_map/all_to_all | solution.py:322
  163.6 32.0 %copy-start.7 = (bf16[20,20]{1,0:T(8,128)(2,1)S(1)}, bf16[20,20]{1,0:T(8,128)(2,1)}, u32[]{:S(2)}) copy-start(bf16[20,20]{1,0:T(8,128)(2,1)} %param.14) | copy-start | bytes 2404
  163.6 47.2 %collective-permute-start.4 = (f32[16,6,24,128]{3,2,1,0:T(8,128)}, f32[16,6,24,128]{3,2,1,0:T(8,128)}, u32[]{:S(2)}, u32[]{:S(2)}) collective-permute-start(f32[16,6,24,128]{3,2,1,0:T(8,128)} %all-to-all-done.4.refs_0_), channel_id=1, source_target_pairs={{0,1},{1,0},{2,3},{3,2},{4,5},{5,4},{6,7},{7,6},{8,9},{9,8},{10,11... | collective-permute-start | bytes 3538952 | tf_op jit(solution)/shard_map/ppermute | solution.py:335
  189.3 6.2 %copy-start.1 = (f32[16,6,24,128]{3,2,1,0:T(8,128)}, f32[16,6,24,128]{3,2,1,0:T(8,128)S(1)}, u32[]{:S(2)}) copy-start(f32[16,6,24,128]{3,2,1,0:T(8,128)S(1)} %all-to-all-done.3.refs_0_) | copy-start | bytes 3538948
  189.3 21.5 %all-to-all-start.2 = ((f32[16,3,24,128]{3,2,1,0:T(8,128)}), f32[16,3,24,128]{3,2,1,0:T(8,128)}, u32[]{:S(2)}, u32[]{:S(2)}) async-start(f32[16,3,24,128]{3,2,1,0:T(8,128)} %mix_x.5), calls=%async_computation.2 | async-start | bytes 1179648 | tf_op jit(solution)/shard_map/all_to_all | solution.py:322
  197.0 2.8 copy-start.5
  197.3 3.1 %copy-start.2 = (f32[16,6,24,128]{3,2,1,0:T(8,128)S(1)}, f32[16,6,24,128]{3,2,1,0:T(8,128)}, u32[]{:S(2)}) copy-start(f32[16,6,24,128]{3,2,1,0:T(8,128)} %copy-done.1) | copy-start | bytes 3538948
  197.4 3.1 %copy-start.6 = (bf16[2,96,192]{2,1,0:T(8,128)(2,1)S(1)}, bf16[2,96,192]{2,1,0:T(8,128)(2,1)}, u32[]{:S(2)}) copy-start(bf16[2,96,192]{2,1,0:T(8,128)(2,1)} %constant.33.clone) | copy-start | bytes 221188
  200.4 34.7 %collective-permute-start.3 = (f32[16,6,24,128]{3,2,1,0:T(8,128)S(1)}, f32[16,6,24,128]{3,2,1,0:T(8,128)S(1)}, u32[]{:S(2)}, u32[]{:S(2)}) collective-permute-start(f32[16,6,24,128]{3,2,1,0:T(8,128)S(1)} %copy-done.2), channel_id=1, source_target_pairs={{0,1},{1,0},{2,3},{3,2},{4,5},{5,4},{6,7},{7,6},{8,9},{9,8},{10,11... | collective-permute-start | bytes 3538952 | tf_op jit(solution)/shard_map/ppermute | solution.py:335
  210.8 49.5 %collective-permute-start.2 = (f32[16,3,24,128]{3,2,1,0:T(8,128)}, f32[16,3,24,128]{3,2,1,0:T(8,128)S(1)}, u32[]{:S(2)}, u32[]{:S(2)}) collective-permute-start(f32[16,3,24,128]{3,2,1,0:T(8,128)} %all-to-all-done.2.refs_0_), channel_id=1, source_target_pairs={{0,1},{1,0},{2,3},{3,2},{4,5},{5,4},{6,7},{7,6},{8,9},{9,8},{10,11... | collective-permute-start | bytes 1769480 | tf_op jit(solution)/shard_map/ppermute | solution.py:335
  235.1 1.1 copy-start.8
  260.3 0.9 copy-start.4

commit v3 on v2

--- a/solution.py
+++ b/solution.py
@@ -46,30 +46,36 @@
 
 
 def forward_kernel(direct, my, units, *refs):
-    fields, (t_ref, z_ref, own_ref, other_ref, g_high, g_low) = refs[:units], refs[units:]
-    per_unit, _, _, nz = fields[0].shape
+    fields, (t_ref, z_ref, own_ref, other_ref), scratch = (
+        refs[:units], refs[units:units + 4], refs[units + 4:])
+    per_unit, count, _, nz = fields[0].shape
     table = t_ref[...]
-    for c in range(units * per_unit):
-        cells = fields[c // per_unit][c % per_unit, 0]
-        high, low = split(dot(table, jnp.concatenate([cells, cells], 0)))
-        rows = slice(c * my, (c + 1) * my)
-        for q in range(2):
-            g_high[rows, q * nz:(q + 1) * nz] = high[q * my:(q + 1) * my]
-            g_low[rows, q * nz:(q + 1) * nz] = low[q * my:(q + 1) * my]
+    for k in range(count):
+        g_high, g_low = scratch[2 * k:2 * k + 2]
+        for c in range(units * per_unit):
+            cells = fields[c // per_unit][c % per_unit, k]
+            high, low = split(dot(table, jnp.concatenate([cells, cells], 0)))
+            rows = slice(c * my, (c + 1) * my)
+            for q in range(2):
+                g_high[rows, q * nz:(q + 1) * nz] = high[q * my:(q + 1) * my]
+                g_low[rows, q * nz:(q + 1) * nz] = low[q * my:(q + 1) * my]
     modes = z_ref.shape[0] // 2
-    first = dot_nt(z_ref[...], g_high[...])
-    out = first[:modes] + first[modes:] + dot_nt(z_ref[:modes], g_low[...])
-    out = jnp.concatenate([out[:modes // 2], out[modes // 2:]], 1)
     half = modes // 4
-    for ref, part in ((own_ref, out[:half]), (other_ref, out[half:])):
-        if direct:
-            tiles, xb = ref.shape[1:3]
-            flat = ref.reshape(half * tiles * xb, 128)
-            for t in range(tiles):
-                flat[pl.ds(t * xb + pl.program_id(1), half, stride=tiles * xb), :] = part[
-                    :, t * 128:(t + 1) * 128]
-        else:
-            ref[0] = part
+    for k in range(count):
+        g_high, g_low = scratch[2 * k:2 * k + 2]
+        first = dot_nt(z_ref[...], g_high[...])
+        out = first[:modes] + first[modes:] + dot_nt(z_ref[:modes], g_low[...])
+        out = jnp.concatenate([out[:modes // 2], out[modes // 2:]], 1)
+        for ref, part in ((own_ref, out[:half]), (other_ref, out[half:])):
+            if direct:
+                tiles, xb = ref.shape[1:3]
+                flat = ref.reshape(half * tiles * xb, 128)
+                at = pl.program_id(1) * count + k
+                for t in range(tiles):
+                    flat[pl.ds(t * xb + at, half, stride=tiles * xb), :] = part[
+                        :, t * 128:(t + 1) * 128]
+            else:
+                ref[0] = part
 
 
 def mix_kernel(units, has_before, last, *refs):
@@ -136,42 +142,46 @@
 
 def inverse_kernel(direct, my, start, chained, *refs):
     (own_ref, other_ref, field_ref, z_ref, t_ref, pw_ref, bias_ref) = refs[:7]
-    out_ref, v_high, v_low, local = refs[7 + chained:]
-    channels, _, ny, nz = field_ref.shape
+    out_ref, scratch = refs[7 + chained], refs[8 + chained:]
+    channels, count, ny, nz = field_ref.shape
     outs = out_ref.shape[0]
+    lanes = outs * my
     group = 16
-    for g in range(0, ny, 2 * group):
-        pair = [field_ref[:, 0, g + k * group:g + (k + 1) * group, :].reshape(channels * group, nz)
-                for k in range(2)]
-        both = dot(pw_ref[...], jnp.concatenate(pair, 1))
-        for k in range(2):
-            local[:, g + k * group:g + (k + 1) * group, :] = both[:, k * nz:(k + 1) * nz].reshape(
-                outs, group, nz)
-    parts = []
-    for ref in (own_ref, other_ref):
-        if direct:
-            half, tiles, xb, _ = ref.shape
-            flat = ref.reshape(half * tiles * xb, 128)
-            parts.append(jnp.concatenate(
-                [flat[pl.ds(t * xb + pl.program_id(1), half, stride=tiles * xb), :]
-                 for t in range(tiles)], 1))
-        else:
-            parts.append(ref[0])
-    wide = jnp.concatenate(parts, 0)
-    lanes = outs * my
-    high, low = split(jnp.concatenate([wide[:, :lanes], wide[:, lanes:2 * lanes]], 0))
-    high, low = split(dot_tn(jnp.concatenate([high, low, high], 0), z_ref[...]))
-    v_high[...] = high
-    v_low[...] = low
+    for k in range(count):
+        v_high, v_low, local = scratch[3 * k:3 * k + 3]
+        parts = []
+        for ref in (own_ref, other_ref):
+            if direct:
+                half, tiles, xb, _ = ref.shape
+                flat = ref.reshape(half * tiles * xb, 128)
+                at = pl.program_id(1) * count + k
+                parts.append(jnp.concatenate(
+                    [flat[pl.ds(t * xb + at, half, stride=tiles * xb), :] for t in range(tiles)], 1))
+            else:
+                parts.append(ref[0])
+        wide = jnp.concatenate(parts, 0)
+        high, low = split(jnp.concatenate([wide[:, :lanes], wide[:, lanes:2 * lanes]], 0))
+        high, low = split(dot_tn(jnp.concatenate([high, low, high], 0), z_ref[...]))
+        v_high[...] = high
+        v_low[...] = low
+        for g in range(0, ny, 2 * group):
+            pair = [field_ref[:, k, g + j * group:g + (j + 1) * group, :].reshape(
+                channels * group, nz) for j in range(2)]
+            both = dot(pw_ref[...], jnp.concatenate(pair, 1))
+            for j in range(2):
+                local[:, g + j * group:g + (j + 1) * group, :] = both[
+                    :, j * nz:(j + 1) * nz].reshape(outs, group, nz)
     taps = 2 * my
-    for c in range(outs):
-        rows = slice(c * my, (c + 1) * my)
-        top = [v_high[rows, q * nz:(q + 1) * nz] for q in range(2)]
-        rest = [v_low[rows, q * nz:(q + 1) * nz] for q in range(2)]
-        total = dot(t_ref[:, :2 * taps], jnp.concatenate(top + top, 0)) + dot(
-            t_ref[:, :taps], jnp.concatenate(rest, 0))
-        total = total + local[c] + bias_ref[start + c]
-        out_ref[c, 0] = jax.nn.gelu(total).astype(BF16)
+    for k in range(count):
+        v_high, v_low, local = scratch[3 * k:3 * k + 3]
+        for c in range(outs):
+            rows = slice(c * my, (c + 1) * my)
+            top = [v_high[rows, q * nz:(q + 1) * nz] for q in range(2)]
+            rest = [v_low[rows, q * nz:(q + 1) * nz] for q in range(2)]
+            total = dot(t_ref[:, :2 * taps], jnp.concatenate(top + top, 0)) + dot(
+                t_ref[:, :taps], jnp.concatenate(rest, 0))
+            total = total + local[c] + bias_ref[start + c]
+            out_ref[c, k] = jax.nn.gelu(total).astype(BF16)
 
 
 def whole_spec(shape):
@@ -230,14 +240,16 @@
 
     cells = field[0]
     xb = 8 if direct else 1
-    grid = (x_local // xb, xb)
+    per_step = 4 if direct else 1
+    grid = (x_local // xb, xb // per_step)
     limit = 60 * 2**20
     params = pltpu.CompilerParams(
         dimension_semantics=("arbitrary", "arbitrary"), vmem_limit_bytes=limit)
     swap = [(0, 1), (1, 0)]
 
     def field_spec(size, at):
-        return pl.BlockSpec((size, 1, y_local, nz), lambda a, b: (at, a * xb + b, 0, 0))
+        return pl.BlockSpec(
+            (size, per_step, y_local, nz), lambda a, b: (at, a * grid[1] + b, 0, 0))
 
     def wide_of(count):
         lanes = 2 * count * my
@@ -257,7 +269,7 @@
             in_specs=[field_spec(per_unit, u) for u in units]
             + [whole_spec(t_forward.shape), whole_spec(z_forward.shape)],
             out_specs=[spec, spec],
-            scratch_shapes=[pltpu.VMEM((count * my, 2 * nz), BF16)] * 2,
+            scratch_shapes=[pltpu.VMEM((count * my, 2 * nz), BF16)] * (2 * per_step),
             compiler_params=params,
             cost_estimate=pl.CostEstimate(
                 flops=count * x_local * 40_000_000, transcendentals=0,
@@ -350,8 +362,8 @@
             grid=grid,
             in_specs=specs,
             out_specs=field_spec(count, first // count),
-            scratch_shapes=[pltpu.VMEM((count * my, 2 * nz), BF16)] * 2
-            + [pltpu.VMEM((count, y_local, nz), F32)],
+            scratch_shapes=([pltpu.VMEM((count * my, 2 * nz), BF16)] * 2
+                            + [pltpu.VMEM((count, y_local, nz), F32)]) * per_step,
             input_output_aliases={7: 0} if chained else {},
             compiler_params=params,
             cost_estimate=pl.CostEstimate(

time: 287 us -> 237 us (0.83)
  Pallas kernels: 151 us -> 96.8 us
  waiting for transfers between devices: 76.7 us -> 84.1 us
    pallas_call x3, Pallas kernels: 70.1 us -> 37.5 us  [to_cells(): pl.pallas_call(functools.partial(inverse_kernel, direct, my, first, int(c...]
    pallas_call x2, Pallas kernels: 42.9 us -> 21.1 us  [to_modes(): pl.pallas_call(functools.partial(forward_kernel, direct, my, len(units)),...]
    all_to_all x2, waiting for transfers between devices: 24.2 us -> 31.4 us  [to_modes(): return lax.all_to_all(summed, 'px', split_axis=0, concat_axis=0, tiled=True)]
  transfers between devices with their start and end apart: 10 -> 10, of which waited for: 6 -> 7; matrix products, arithmetic and copies ran while one was open for 3% -> 4% of each run, Pallas kernels for 36% -> 29%
where the time goes in v3:
time: 237 us; the launch traced here: 235 us
  Pallas kernels  96.8 us (41%)
  waiting for transfers between devices  84.1 us (35%)
  starting transfers between devices  36.3 us (15%)
  local copies, waits for them, and re-layouts  12.1 us (5%)
  other arithmetic  5.75 us (2%)
    all_to_all x3, waiting for transfers between devices, send_back(): return lax.all_to_all(mixed, 'px', split_axis=0, concat_axis=0, tiled=True)  46.1 us
    pallas_call x4, Pallas kernels, mix(): pl.pallas_call(functools.partial(mix_kernel, len(units), before is not No...  38.2 us
    pallas_call x3, Pallas kernels, to_cells(): pl.pallas_call(functools.partial(inverse_kernel, direct, my, first, int(c...  37.5 us
    all_to_all x2, waiting for transfers between devices, to_modes(): return lax.all_to_all(summed, 'px', split_axis=0, concat_axis=0, tiled=True)  31.4 us
    pallas_call x2, Pallas kernels, to_modes(): pl.pallas_call(functools.partial(forward_kernel, direct, my, len(units)),...  21.1 us
    all_to_all x3, starting transfers between devices, send_back(): return lax.all_to_all(mixed, 'px', split_axis=0, concat_axis=0, tiled=True)  20.7 us
    all_to_all x2, starting transfers between devices, to_modes(): return lax.all_to_all(summed, 'px', split_axis=0, concat_axis=0, tiled=True)  15 us
    ppermute x2, waiting for transfers between devices, to_modes(): summed = own + lax.ppermute(other, 'py', swap)  6.58 us
  transfers between devices with their start and end apart: 10, of which 7 were waited for; matrix products, arithmetic and copies ran while one was open for 4% of the time, Pallas kernels for 29%

profile of v3, /device:TPU:0, one launch (start us, length us, event | category | flops | bytes accessed | tf_op | source)
XLA Modules:
  0.0 235.3 jit_solution(16592924555766321323)
XLA Ops:
  0.0 1.4 dynamic-slice_bitcast_fusion.3.refs_3_.refs_2_
  1.4 1.5 dynamic-slice_bitcast_fusion.1.refs_4_.refs_3_
  2.9 9.1 %forward_yz.3 = (f32[16,6,24,128]{3,2,1,0:T(8,128)}, f32[16,6,24,128]{3,2,1,0:T(8,128)}) custom-call(bf16[20,24,96,128]{3,2,1,0:T(8,128)(2,1)} %bitcast.22, bf16[20,24,96,128]{3,2,1,0:T(8,128)(2,1)} %bitcast.23, bf16[96,192]{1,0:T(8,128)(2,1)} %dynamic-slice_bitcast_fusion.3.refs_3_.refs_2_, bf16[128,256]{1,0:T(8,128)(2,1)} %dynamic-slice_bitcast_fusion.1.refs_4_.refs_3_), custom_call_target="tpu_custom_call" | custom-call | flops 7680000000 | bytes 9437184 | tf_op jit(solution)/shard_map/forward_yz/pallas_call | solution.py:264
  12.5 2.7 %collective-permute-done.1 = f32[16,6,24,128]{3,2,1,0:T(8,128)S(1)} collective-permute-done((f32[16,6,24,128]{3,2,1,0:T(8,128)}, f32[16,6,24,128]{3,2,1,0:T(8,128)S(1)}, u32[]{:S(2)}, u32[]{:S(2)}) %collective-permute-start.1) | collective-permute-done | bytes 1179680 | tf_op jit(solution)/shard_map/ppermute | solution.py:278
  15.2 2.4 %add.17 = f32[16,6,24,128]{3,2,1,0:T(8,128)} add(f32[16,6,24,128]{3,2,1,0:T(8,128)} %get-tuple-element.11, f32[16,6,24,128]{3,2,1,0:T(8,128)S(1)} %collective-permute-done.1) | non-fusion elementwise | flops 294912 | bytes 3538944 | tf_op jit(solution)/shard_map/add | solution.py:278
  17.7 8.2 %all-to-all-start.1 = ((f32[16,6,24,128]{3,2,1,0:T(8,128)}), f32[16,6,24,128]{3,2,1,0:T(8,128)S(1)}, u32[]{:S(2)}, u32[]{:S(2)}) async-start(f32[16,6,24,128]{3,2,1,0:T(8,128)} %add.17), calls=%async_computation.1 | async-start | bytes 2359296 | tf_op jit(solution)/shard_map/all_to_all | solution.py:280
  25.9 12.0 %forward_yz.2 = (f32[16,9,24,128]{3,2,1,0:T(8,128)}, f32[16,9,24,128]{3,2,1,0:T(8,128)}) custom-call(bf16[20,24,96,128]{3,2,1,0:T(8,128)(2,1)} %bitcast.24, bf16[20,24,96,128]{3,2,1,0:T(8,128)(2,1)} %bitcast.25, bf16[20,24,96,128]{3,2,1,0:T(8,128)(2,1)} %bitcast.26, bf16[96,192]{1,0:T(8,128)(2,1)} %dynamic-slice_bitcast_fusion.3.refs_3_.refs_2_, ...), custom_call_target="tpu_custom_call" | custom-call | flops 11520000000 | bytes 14155776 | tf_op jit(solution)/shard_map/forward_yz/pallas_call | solution.py:264
  37.9 3.9 %collective-permute-done = f32[16,9,24,128]{3,2,1,0:T(8,128)S(1)} collective-permute-done((f32[16,9,24,128]{3,2,1,0:T(8,128)}, f32[16,9,24,128]{3,2,1,0:T(8,128)S(1)}, u32[]{:S(2)}, u32[]{:S(2)}) %collective-permute-start) | collective-permute-done | bytes 1769504 | tf_op jit(solution)/shard_map/ppermute | solution.py:278
  41.8 2.9 %add.16 = f32[16,9,24,128]{3,2,1,0:T(8,128)} add(f32[16,9,24,128]{3,2,1,0:T(8,128)} %get-tuple-element.9, f32[16,9,24,128]{3,2,1,0:T(8,128)S(1)} %collective-permute-done) | non-fusion elementwise | flops 442368 | bytes 5308416 | tf_op jit(solution)/shard_map/add | solution.py:278
  44.7 8.3 %all-to-all-done.1.refs_0_ = f32[16,6,24,128]{3,2,1,0:T(8,128)S(1)} async-done(((f32[16,6,24,128]{3,2,1,0:T(8,128)}), f32[16,6,24,128]{3,2,1,0:T(8,128)S(1)}, u32[]{:S(2)}, u32[]{:S(2)}) %all-to-all-start.1) | async-done | bytes 1179680 | tf_op jit(solution)/shard_map/all_to_all | solution.py:280
  53.0 1.1 copy-done.3
  54.0 6.8 %all-to-all-start = ((f32[16,9,24,128]{3,2,1,0:T(8,128)}), f32[16,9,24,128]{3,2,1,0:T(8,128)S(1)}, u32[]{:S(2)}, u32[]{:S(2)}) async-start(f32[16,9,24,128]{3,2,1,0:T(8,128)} %add.16), calls=%async_computation | async-start | bytes 3538944 | tf_op jit(solution)/shard_map/all_to_all | solution.py:280
  60.9 13.5 %mix_x.4.refs_6_ = f32[20,2,48,96]{3,2,1,0:T(8,128)} custom-call(f32[16,6,24,128]{3,2,1,0:T(8,128)} %copy-done.3, bf16[768,256]{1,0:T(8,128)(2,1)} %constant.36.clone.refs_1_.refs_7_, bf16[768,256]{1,0:T(8,128)(2,1)} %constant.37.clone.refs_2_.refs_8_, bf16[2,20,20,48,96]{4,3,2,1,0:T(8,128)(2,1)} %refs_5_.5, bf16[2,20,20,48,96]{4,3,2,1,0:T(8,128)(2,1)} %refs_5_.5), custom_call_target="tpu_custom_call" | custom-call | flops 6400000000 | bytes 3932160 | tf_op jit(solution)/shard_map/mix_x/pallas_call | solution.py:317
  74.3 23.1 %all-to-all-done.refs_0_ = f32[16,9,24,128]{3,2,1,0:T(8,128)S(1)} async-done(((f32[16,9,24,128]{3,2,1,0:T(8,128)}), f32[16,9,24,128]{3,2,1,0:T(8,128)S(1)}, u32[]{:S(2)}, u32[]{:S(2)}) %all-to-all-start) | async-done | bytes 1769504 | tf_op jit(solution)/shard_map/all_to_all | solution.py:280
  97.4 1.2 copy-done
  98.6 9.2 %mix_x.7 = f32[16,6,24,128]{3,2,1,0:T(8,128)} custom-call(f32[16,9,24,128]{3,2,1,0:T(8,128)} %copy-done, bf16[768,256]{1,0:T(8,128)(2,1)} %constant.36.clone.refs_1_.refs_7_, bf16[768,256]{1,0:T(8,128)(2,1)} %constant.37.clone.refs_2_.refs_8_, bf16[2,20,20,48,96]{4,3,2,1,0:T(8,128)(2,1)} %refs_5_.5, bf16[2,20,20,48,96]{4,3,2,1,0:T(8,128)(2,1)} %refs_5_.5, ...), custom_call_target="tpu_custom_call" | custom-call | flops 3840000000 | bytes 2359296 | tf_op jit(solution)/shard_map/mix_x/pallas_call | solution.py:317
  107.8 8.3 %all-to-all-start.4 = ((f32[16,6,24,128]{3,2,1,0:T(8,128)}), f32[16,6,24,128]{3,2,1,0:T(8,128)}, u32[]{:S(2)}, u32[]{:S(2)}) async-start(f32[16,6,24,128]{3,2,1,0:T(8,128)} %mix_x.7), calls=%async_computation.4 | async-start | bytes 2359296 | tf_op jit(solution)/shard_map/all_to_all | solution.py:334
  116.1 9.2 %mix_x.6 = f32[16,6,24,128]{3,2,1,0:T(8,128)} custom-call(f32[16,9,24,128]{3,2,1,0:T(8,128)} %copy-done, bf16[768,256]{1,0:T(8,128)(2,1)} %constant.36.clone.refs_1_.refs_7_, bf16[768,256]{1,0:T(8,128)(2,1)} %constant.37.clone.refs_2_.refs_8_, bf16[2,20,20,48,96]{4,3,2,1,0:T(8,128)(2,1)} %refs_5_.5, bf16[2,20,20,48,96]{4,3,2,1,0:T(8,128)(2,1)} %refs_5_.5, ...), custom_call_target="tpu_custom_call" | custom-call | flops 3840000000 | bytes 2359296 | tf_op jit(solution)/shard_map/mix_x/pallas_call | solution.py:317
  125.3 17.0 %all-to-all-done.4.refs_0_ = f32[16,6,24,128]{3,2,1,0:T(8,128)} async-done(((f32[16,6,24,128]{3,2,1,0:T(8,128)}), f32[16,6,24,128]{3,2,1,0:T(8,128)}, u32[]{:S(2)}, u32[]{:S(2)}) %all-to-all-start.4) | async-done | bytes 1179680 | tf_op jit(solution)/shard_map/all_to_all | solution.py:334
  142.3 6.2 %all-to-all-start.3 = ((f32[16,6,24,128]{3,2,1,0:T(8,128)}), f32[16,6,24,128]{3,2,1,0:T(8,128)S(1)}, u32[]{:S(2)}, u32[]{:S(2)}) async-start(f32[16,6,24,128]{3,2,1,0:T(8,128)} %mix_x.6), calls=%async_computation.3 | async-start | bytes 2359296 | tf_op jit(solution)/shard_map/all_to_all | solution.py:334
  148.6 6.4 %mix_x.5 = f32[16,3,24,128]{3,2,1,0:T(8,128)} custom-call(f32[16,9,24,128]{3,2,1,0:T(8,128)} %copy-done, bf16[768,256]{1,0:T(8,128)(2,1)} %constant.36.clone.refs_1_.refs_7_, bf16[768,256]{1,0:T(8,128)(2,1)} %constant.37.clone.refs_2_.refs_8_, bf16[2,20,20,48,96]{4,3,2,1,0:T(8,128)(2,1)} %refs_5_.5, bf16[2,20,20,48,96]{4,3,2,1,0:T(8,128)(2,1)} %refs_5_.5, ...), custom_call_target="tpu_custom_call" | custom-call | flops 1920000000 | bytes 1179648 | tf_op jit(solution)/shard_map/mix_x/pallas_call | solution.py:317
  155.0 19.4 %all-to-all-done.3.refs_0_ = f32[16,6,24,128]{3,2,1,0:T(8,128)S(1)} async-done(((f32[16,6,24,128]{3,2,1,0:T(8,128)}), f32[16,6,24,128]{3,2,1,0:T(8,128)S(1)}, u32[]{:S(2)}, u32[]{:S(2)}) %all-to-all-start.3) | async-done | bytes 1179680 | tf_op jit(solution)/shard_map/all_to_all | solution.py:334
  174.4 6.2 %all-to-all-start.2 = ((f32[16,3,24,128]{3,2,1,0:T(8,128)}), f32[16,3,24,128]{3,2,1,0:T(8,128)}, u32[]{:S(2)}, u32[]{:S(2)}) async-start(f32[16,3,24,128]{3,2,1,0:T(8,128)} %mix_x.5), calls=%async_computation.2 | async-start | bytes 1179648 | tf_op jit(solution)/shard_map/all_to_all | solution.py:334
  181.4 0.7 copy.18.refs_5_
  182.9 0.8 copy.16.refs_5_
  184.1 0.8 copy.17.refs_5_
  186.2 9.7 %all-to-all-done.2.refs_0_ = f32[16,3,24,128]{3,2,1,0:T(8,128)} async-done(((f32[16,3,24,128]{3,2,1,0:T(8,128)}), f32[16,3,24,128]{3,2,1,0:T(8,128)}, u32[]{:S(2)}, u32[]{:S(2)}) %all-to-all-start.2) | async-done | bytes 589856 | tf_op jit(solution)/shard_map/all_to_all | solution.py:334
  195.9 13.3 %inverse_zy.3.refs_7_ = bf16[20,24,96,128]{3,2,1,0:T(8,128)(2,1)} custom-call(f32[16,6,24,128]{3,2,1,0:T(8,128)} %all-to-all-done.4.refs_0_, f32[16,6,24,128]{3,2,1,0:T(8,128)} %collective-permute-done.4.refs_1_, bf16[20,24,96,128]{3,2,1,0:T(8,128)(2,1)} %bitcast.27, bf16[192,256]{1,0:T(8,128)(2,1)} %dynamic-slice_bitcast_fusion.refs_3_, ...), custom_call_target="tpu_custom_call" | custom-call | flops 11520000000 | bytes 14155776 | tf_op jit(solution)/shard_map/inverse_zy/pallas_call | solution.py:358
  209.2 1.0 copy-done.8
  210.3 13.3 %inverse_zy.4.refs_7_ = bf16[20,24,96,128]{3,2,1,0:T(8,128)(2,1)} custom-call(f32[16,6,24,128]{3,2,1,0:T(8,128)} %copy-done.1, f32[16,6,24,128]{3,2,1,0:T(8,128)} %copy-done.8, bf16[20,24,96,128]{3,2,1,0:T(8,128)(2,1)} %bitcast.28, bf16[192,256]{1,0:T(8,128)(2,1)} %dynamic-slice_bitcast_fusion.refs_3_, ...), custom_call_target="tpu_custom_call", output_to_operand_aliasing={{}: (7, {})} | custom-call | flops 11520000000 | bytes 14155776 | tf_op jit(solution)/shard_map/inverse_zy/pallas_call | solution.py:358
  223.6 0.8 copy-done.4
  224.5 10.8 %inverse_zy.5 = bf16[20,24,96,128]{3,2,1,0:T(8,128)(2,1)} custom-call(f32[16,3,24,128]{3,2,1,0:T(8,128)} %all-to-all-done.2.refs_0_, f32[16,3,24,128]{3,2,1,0:T(8,128)} %copy-done.4, bf16[20,24,96,128]{3,2,1,0:T(8,128)(2,1)} %bitcast.29, bf16[192,256]{1,0:T(8,128)(2,1)} %dynamic-slice_bitcast_fusion.refs_3_, ...), custom_call_target="tpu_custom_call", output_to_operand_aliasing={{}: (7, {})} | custom-call | flops 5760000000 | bytes 7077888 | tf_op jit(solution)/shard_map/inverse_zy/pallas_call | solution.py:358
  (32 shorter events, 3.8 us)
Async XLA Ops:
  12.0 3.2 %collective-permute-start.1 = (f32[16,6,24,128]{3,2,1,0:T(8,128)}, f32[16,6,24,128]{3,2,1,0:T(8,128)S(1)}, u32[]{:S(2)}, u32[]{:S(2)}) collective-permute-start(f32[16,6,24,128]{3,2,1,0:T(8,128)} %get-tuple-element.12), channel_id=1, source_target_pairs={{0,1},{1,0},{2,3},{3,2},{4,5},{5,4},{6,7},{7,6},{8,9},{9,8},{10,11... | collective-permute-start | bytes 3538952 | tf_op jit(solution)/shard_map/ppermute | solution.py:278
  17.7 35.3 %all-to-all-start.1 = ((f32[16,6,24,128]{3,2,1,0:T(8,128)}), f32[16,6,24,128]{3,2,1,0:T(8,128)S(1)}, u32[]{:S(2)}, u32[]{:S(2)}) async-start(f32[16,6,24,128]{3,2,1,0:T(8,128)} %add.17), calls=%async_computation.1 | async-start | bytes 2359296 | tf_op jit(solution)/shard_map/all_to_all | solution.py:280
  37.9 3.9 %collective-permute-start = (f32[16,9,24,128]{3,2,1,0:T(8,128)}, f32[16,9,24,128]{3,2,1,0:T(8,128)S(1)}, u32[]{:S(2)}, u32[]{:S(2)}) collective-permute-start(f32[16,9,24,128]{3,2,1,0:T(8,128)} %get-tuple-element.10), channel_id=1, source_target_pairs={{0,1},{1,0},{2,3},{3,2},{4,5},{5,4},{6,7},{7,6},{8,9},{9,8},{10,11... | collective-permute-start | bytes 5308424 | tf_op jit(solution)/shard_map/ppermute | solution.py:278
  53.0 1.1 copy-start.3
  54.0 43.4 %all-to-all-start = ((f32[16,9,24,128]{3,2,1,0:T(8,128)}), f32[16,9,24,128]{3,2,1,0:T(8,128)S(1)}, u32[]{:S(2)}, u32[]{:S(2)}) async-start(f32[16,9,24,128]{3,2,1,0:T(8,128)} %add.16), calls=%async_computation | async-start | bytes 3538944 | tf_op jit(solution)/shard_map/all_to_all | solution.py:280
  97.4 1.2 copy-start
  107.8 34.5 %all-to-all-start.4 = ((f32[16,6,24,128]{3,2,1,0:T(8,128)}), f32[16,6,24,128]{3,2,1,0:T(8,128)}, u32[]{:S(2)}, u32[]{:S(2)}) async-start(f32[16,6,24,128]{3,2,1,0:T(8,128)} %mix_x.7), calls=%async_computation.4 | async-start | bytes 2359296 | tf_op jit(solution)/shard_map/all_to_all | solution.py:334
  142.3 32.0 %all-to-all-start.3 = ((f32[16,6,24,128]{3,2,1,0:T(8,128)}), f32[16,6,24,128]{3,2,1,0:T(8,128)S(1)}, u32[]{:S(2)}, u32[]{:S(2)}) async-start(f32[16,6,24,128]{3,2,1,0:T(8,128)} %mix_x.6), calls=%async_computation.3 | async-start | bytes 2359296 | tf_op jit(solution)/shard_map/all_to_all | solution.py:334
  148.5 32.1 %copy-start.7 = (bf16[20,20]{1,0:T(8,128)(2,1)S(1)}, bf16[20,20]{1,0:T(8,128)(2,1)}, u32[]{:S(2)}) copy-start(bf16[20,20]{1,0:T(8,128)(2,1)} %param.14) | copy-start | bytes 2404
  148.5 47.4 %collective-permute-start.4 = (f32[16,6,24,128]{3,2,1,0:T(8,128)}, f32[16,6,24,128]{3,2,1,0:T(8,128)}, u32[]{:S(2)}, u32[]{:S(2)}) collective-permute-start(f32[16,6,24,128]{3,2,1,0:T(8,128)} %all-to-all-done.4.refs_0_), channel_id=1, source_target_pairs={{0,1},{1,0},{2,3},{3,2},{4,5},{5,4},{6,7},{7,6},{8,9},{9,8},{10,11... | collective-permute-start | bytes 3538952 | tf_op jit(solution)/shard_map/ppermute | solution.py:347
  174.4 6.3 %copy-start.1 = (f32[16,6,24,128]{3,2,1,0:T(8,128)}, f32[16,6,24,128]{3,2,1,0:T(8,128)S(1)}, u32[]{:S(2)}) copy-start(f32[16,6,24,128]{3,2,1,0:T(8,128)S(1)} %all-to-all-done.3.refs_0_) | copy-start | bytes 3538948
  174.4 21.5 %all-to-all-start.2 = ((f32[16,3,24,128]{3,2,1,0:T(8,128)}), f32[16,3,24,128]{3,2,1,0:T(8,128)}, u32[]{:S(2)}, u32[]{:S(2)}) async-start(f32[16,3,24,128]{3,2,1,0:T(8,128)} %mix_x.5), calls=%async_computation.2 | async-start | bytes 1179648 | tf_op jit(solution)/shard_map/all_to_all | solution.py:334
  182.1 2.8 %copy-start.5 = (bf16[2,192,256]{2,1,0:T(8,128)(2,1)S(1)}, bf16[2,192,256]{2,1,0:T(8,128)(2,1)}, u32[]{:S(2)}) copy-start(bf16[2,192,256]{2,1,0:T(8,128)(2,1)} %constant.35.clone) | copy-start | bytes 589828
  182.5 3.1 %copy-start.2 = (f32[16,6,24,128]{3,2,1,0:T(8,128)S(1)}, f32[16,6,24,128]{3,2,1,0:T(8,128)}, u32[]{:S(2)}) copy-start(f32[16,6,24,128]{3,2,1,0:T(8,128)} %copy-done.1) | copy-start | bytes 3538948
  182.5 3.1 %copy-start.6 = (bf16[2,96,192]{2,1,0:T(8,128)(2,1)S(1)}, bf16[2,96,192]{2,1,0:T(8,128)(2,1)}, u32[]{:S(2)}) copy-start(bf16[2,96,192]{2,1,0:T(8,128)(2,1)} %constant.33.clone) | copy-start | bytes 221188
  185.5 23.7 %collective-permute-start.3 = (f32[16,6,24,128]{3,2,1,0:T(8,128)S(1)}, f32[16,6,24,128]{3,2,1,0:T(8,128)S(1)}, u32[]{:S(2)}, u32[]{:S(2)}) collective-permute-start(f32[16,6,24,128]{3,2,1,0:T(8,128)S(1)} %copy-done.2), channel_id=1, source_target_pairs={{0,1},{1,0},{2,3},{3,2},{4,5},{5,4},{6,7},{7,6},{8,9},{9,8},{10,11... | collective-permute-start | bytes 3538952 | tf_op jit(solution)/shard_map/ppermute | solution.py:347
  195.9 27.7 %collective-permute-start.2 = (f32[16,3,24,128]{3,2,1,0:T(8,128)}, f32[16,3,24,128]{3,2,1,0:T(8,128)S(1)}, u32[]{:S(2)}, u32[]{:S(2)}) collective-permute-start(f32[16,3,24,128]{3,2,1,0:T(8,128)} %all-to-all-done.2.refs_0_), channel_id=1, source_target_pairs={{0,1},{1,0},{2,3},{3,2},{4,5},{5,4},{6,7},{7,6},{8,9},{9,8},{10,11... | collective-permute-start | bytes 1769480 | tf_op jit(solution)/shard_map/ppermute | solution.py:347
  209.2 1.1 copy-start.8
  223.6 0.9 copy-start.4

commit v4 on v3

--- a/solution.py
+++ b/solution.py
@@ -49,7 +49,9 @@
     fields, (t_ref, z_ref, own_ref, other_ref), scratch = (
         refs[:units], refs[units:units + 4], refs[units + 4:])
     per_unit, count, _, nz = fields[0].shape
-    table = t_ref[...]
+    py = lax.axis_index("py")
+    table = t_ref[py]
+    z_ref = z_ref.at[py]
     for k in range(count):
         g_high, g_low = scratch[2 * k:2 * k + 2]
         for c in range(units * per_unit):
@@ -143,6 +145,8 @@
 def inverse_kernel(direct, my, start, chained, *refs):
     (own_ref, other_ref, field_ref, z_ref, t_ref, pw_ref, bias_ref) = refs[:7]
     out_ref, scratch = refs[7 + chained], refs[8 + chained:]
+    py = lax.axis_index("py")
+    t_ref, z_ref = t_ref.at[py], z_ref.at[py]
     channels, count, ny, nz = field_ref.shape
     outs = out_ref.shape[0]
     lanes = outs * my
@@ -194,7 +198,6 @@
     npx, npy = lax.axis_size("px"), lax.axis_size("py")
     assert samples == 1 and npy == 2
     nx, ny = x_local * npx, y_local * npy
-    py = lax.axis_index("py")
     modes = spectral_weight.shape[3]
     per_kz = my // modes
     held = -(-modes // 16) * 16
@@ -224,7 +227,7 @@
         high, low = split_np(rows)
         z_back.append(np.concatenate([high, high, low], 0))
     t_forward, t_back, z_forward, z_back = [
-        lax.dynamic_index_in_dim(jnp.asarray(np.stack(table)), py, 0, keepdims=False)
+        jnp.asarray(np.stack(table))
         for table in (t_forward, t_back, z_forward, z_back)]
 
     x_angle = angles(kept(nx, mx), np.arange(nx), nx).T
@@ -346,10 +349,10 @@
         first = units[0] * per_unit
         partner = lax.ppermute(back, "py", swap)
         _, spec = wide_of(count)
-        weights = kron[first * 16:(first + count) * 16]
-        operands = [back, partner, cells, z_back, t_back, weights, bias]
+        operands = [back, partner, cells, z_back, t_back, kron, bias]
         specs = [spec, spec, field_spec(channels, 0), whole_spec(z_back.shape),
-                 whole_spec(t_back.shape), whole_spec(weights.shape),
+                 whole_spec(t_back.shape),
+                 pl.BlockSpec((count * 16, channels * 16), lambda a, b: (first // count, 0)),
                  pl.BlockSpec(memory_space=pltpu.SMEM)]
         chained = so_far is not None
         if chained:

time: 237 us -> 234 us (0.987)
  local copies, waits for them, and re-layouts: 12.1 us -> 5.02 us
  waiting for transfers between devices: 84.1 us -> 87.4 us
    squeeze x4 -> x0, local copies, waits for them, and re-layouts: 4.17 us -> none  [per_device(): lax.dynamic_index_in_dim(jnp.asarray(np.stack(table)), py, 0, keepdims=Fa...]
    slice x8 -> x0, local copies, waits for them, and re-layouts: 3.76 us -> none  [to_cells(): weights = kron[first * 16:(first + count) * 16]]
    all_to_all x3, waiting for transfers between devices: 46.1 us -> 49.5 us  [send_back(): return lax.all_to_all(mixed, 'px', split_axis=0, concat_axis=0, tiled=True)]
  transfers between devices with their start and end apart: 10 -> 10, of which waited for: 7 -> 7; matrix products, arithmetic and copies ran while one was open for 4% -> 2% of each run, Pallas kernels for 29% -> 29%
where the time goes in v4:
time: 234 us; the launch traced here: 232 us
  Pallas kernels  97.1 us (41%)
  waiting for transfers between devices  87.4 us (37%)
  starting transfers between devices  36.6 us (16%)
  other arithmetic  5.75 us (2%)
  local copies, waits for them, and re-layouts  5.02 us (2%)
    all_to_all x3, waiting for transfers between devices, send_back(): return lax.all_to_all(mixed, 'px', split_axis=0, concat_axis=0, tiled=True)  49.5 us
    pallas_call x4, Pallas kernels, mix(): pl.pallas_call(functools.partial(mix_kernel, len(units), before is not No...  38.2 us
    pallas_call x3, Pallas kernels, to_cells(): pl.pallas_call(functools.partial(inverse_kernel, direct, my, first, int(c...  37.7 us
    all_to_all x2, waiting for transfers between devices, to_modes(): return lax.all_to_all(summed, 'px', split_axis=0, concat_axis=0, tiled=True)  31.4 us
    pallas_call x2, Pallas kernels, to_modes(): pl.pallas_call(functools.partial(forward_kernel, direct, my, len(units)),...  21.1 us
    all_to_all x3, starting transfers between devices, send_back(): return lax.all_to_all(mixed, 'px', split_axis=0, concat_axis=0, tiled=True)  20.9 us
    all_to_all x2, starting transfers between devices, to_modes(): return lax.all_to_all(summed, 'px', split_axis=0, concat_axis=0, tiled=True)  15 us
    ppermute x2, waiting for transfers between devices, to_modes(): summed = own + lax.ppermute(other, 'py', swap)  6.58 us
  transfers between devices with their start and end apart: 10, of which 7 were waited for; matrix products, arithmetic and copies ran while one was open for 2% of the time, Pallas kernels for 29%

profile of v4, /device:TPU:0, one launch (start us, length us, event | category | flops | bytes accessed | tf_op | source)
XLA Modules:
  0.0 232.0 jit_solution(17458122797472737485)
XLA Ops:
  0.0 9.2 %forward_yz.3 = (f32[16,6,24,128]{3,2,1,0:T(8,128)}, f32[16,6,24,128]{3,2,1,0:T(8,128)}) custom-call(bf16[20,24,96,128]{3,2,1,0:T(8,128)(2,1)} %bitcast.4, bf16[20,24,96,128]{3,2,1,0:T(8,128)(2,1)} %bitcast.5, bf16[2,96,192]{2,1,0:T(8,128)(2,1)} %constant.12.clone.refs_3_.refs_2_, bf16[2,128,256]{2,1,0:T(8,128)(2,1)} %constant.14.clone.refs_4_.refs_3_), custom_call_target="tpu_custom_call" | custom-call | flops 7680000000 | bytes 9437184 | tf_op jit(solution)/shard_map/forward_yz/pallas_call | solution.py:267
  9.2 0.5 collective-permute-start.1
  9.7 2.7 %collective-permute-done.1 = f32[16,6,24,128]{3,2,1,0:T(8,128)S(1)} collective-permute-done((f32[16,6,24,128]{3,2,1,0:T(8,128)}, f32[16,6,24,128]{3,2,1,0:T(8,128)S(1)}, u32[]{:S(2)}, u32[]{:S(2)}) %collective-permute-start.1) | collective-permute-done | bytes 1179680 | tf_op jit(solution)/shard_map/ppermute | solution.py:281
  12.4 2.5 %add.7 = f32[16,6,24,128]{3,2,1,0:T(8,128)} add(f32[16,6,24,128]{3,2,1,0:T(8,128)} %get-tuple-element.11, f32[16,6,24,128]{3,2,1,0:T(8,128)S(1)} %collective-permute-done.1) | non-fusion elementwise | flops 294912 | bytes 3538944 | tf_op jit(solution)/shard_map/add | solution.py:281
  14.8 8.2 %all-to-all-start.1 = ((f32[16,6,24,128]{3,2,1,0:T(8,128)}), f32[16,6,24,128]{3,2,1,0:T(8,128)S(1)}, u32[]{:S(2)}, u32[]{:S(2)}) async-start(f32[16,6,24,128]{3,2,1,0:T(8,128)} %add.7), calls=%async_computation.1 | async-start | bytes 2359296 | tf_op jit(solution)/shard_map/all_to_all | solution.py:283
  23.0 12.0 %forward_yz.2 = (f32[16,9,24,128]{3,2,1,0:T(8,128)}, f32[16,9,24,128]{3,2,1,0:T(8,128)}) custom-call(bf16[20,24,96,128]{3,2,1,0:T(8,128)(2,1)} %bitcast.6, bf16[20,24,96,128]{3,2,1,0:T(8,128)(2,1)} %bitcast.7, bf16[20,24,96,128]{3,2,1,0:T(8,128)(2,1)} %bitcast.8, bf16[2,96,192]{2,1,0:T(8,128)(2,1)} %constant.12.clone.refs_3_.refs_2_, ...), custom_call_target="tpu_custom_call" | custom-call | flops 11520000000 | bytes 14155776 | tf_op jit(solution)/shard_map/forward_yz/pallas_call | solution.py:267
  35.0 3.9 %collective-permute-done = f32[16,9,24,128]{3,2,1,0:T(8,128)S(1)} collective-permute-done((f32[16,9,24,128]{3,2,1,0:T(8,128)}, f32[16,9,24,128]{3,2,1,0:T(8,128)S(1)}, u32[]{:S(2)}, u32[]{:S(2)}) %collective-permute-start) | collective-permute-done | bytes 1769504 | tf_op jit(solution)/shard_map/ppermute | solution.py:281
  38.9 2.9 %add.6 = f32[16,9,24,128]{3,2,1,0:T(8,128)} add(f32[16,9,24,128]{3,2,1,0:T(8,128)} %get-tuple-element.9, f32[16,9,24,128]{3,2,1,0:T(8,128)S(1)} %collective-permute-done) | non-fusion elementwise | flops 442368 | bytes 5308416 | tf_op jit(solution)/shard_map/add | solution.py:281
  41.9 8.3 %all-to-all-done.1.refs_0_ = f32[16,6,24,128]{3,2,1,0:T(8,128)S(1)} async-done(((f32[16,6,24,128]{3,2,1,0:T(8,128)}), f32[16,6,24,128]{3,2,1,0:T(8,128)S(1)}, u32[]{:S(2)}, u32[]{:S(2)}) %all-to-all-start.1) | async-done | bytes 1179680 | tf_op jit(solution)/shard_map/all_to_all | solution.py:283
  50.1 1.0 copy-done.2
  51.2 6.8 %all-to-all-start = ((f32[16,9,24,128]{3,2,1,0:T(8,128)}), f32[16,9,24,128]{3,2,1,0:T(8,128)S(1)}, u32[]{:S(2)}, u32[]{:S(2)}) async-start(f32[16,9,24,128]{3,2,1,0:T(8,128)} %add.6), calls=%async_computation | async-start | bytes 3538944 | tf_op jit(solution)/shard_map/all_to_all | solution.py:283
  58.0 13.5 %mix_x.4.refs_6_ = f32[20,2,48,96]{3,2,1,0:T(8,128)} custom-call(f32[16,6,24,128]{3,2,1,0:T(8,128)} %copy-done.2, bf16[768,256]{1,0:T(8,128)(2,1)} %constant.16.clone.refs_1_.refs_7_, bf16[768,256]{1,0:T(8,128)(2,1)} %constant.17.clone.refs_2_.refs_8_, bf16[2,20,20,48,96]{4,3,2,1,0:T(8,128)(2,1)} %refs_5_.5, bf16[2,20,20,48,96]{4,3,2,1,0:T(8,128)(2,1)} %refs_5_.5), custom_call_target="tpu_custom_call" | custom-call | flops 6400000000 | bytes 3932160 | tf_op jit(solution)/shard_map/mix_x/pallas_call | solution.py:320
  71.5 23.1 %all-to-all-done.refs_0_ = f32[16,9,24,128]{3,2,1,0:T(8,128)S(1)} async-done(((f32[16,9,24,128]{3,2,1,0:T(8,128)}), f32[16,9,24,128]{3,2,1,0:T(8,128)S(1)}, u32[]{:S(2)}, u32[]{:S(2)}) %all-to-all-start) | async-done | bytes 1769504 | tf_op jit(solution)/shard_map/all_to_all | solution.py:283
  94.5 1.2 copy-done
  95.8 9.2 %mix_x.7 = f32[16,6,24,128]{3,2,1,0:T(8,128)} custom-call(f32[16,9,24,128]{3,2,1,0:T(8,128)} %copy-done, bf16[768,256]{1,0:T(8,128)(2,1)} %constant.16.clone.refs_1_.refs_7_, bf16[768,256]{1,0:T(8,128)(2,1)} %constant.17.clone.refs_2_.refs_8_, bf16[2,20,20,48,96]{4,3,2,1,0:T(8,128)(2,1)} %refs_5_.5, bf16[2,20,20,48,96]{4,3,2,1,0:T(8,128)(2,1)} %refs_5_.5, ...), custom_call_target="tpu_custom_call" | custom-call | flops 3840000000 | bytes 2359296 | tf_op jit(solution)/shard_map/mix_x/pallas_call | solution.py:320
  104.9 8.3 %all-to-all-start.4 = ((f32[16,6,24,128]{3,2,1,0:T(8,128)}), f32[16,6,24,128]{3,2,1,0:T(8,128)}, u32[]{:S(2)}, u32[]{:S(2)}) async-start(f32[16,6,24,128]{3,2,1,0:T(8,128)} %mix_x.7), calls=%async_computation.4 | async-start | bytes 2359296 | tf_op jit(solution)/shard_map/all_to_all | solution.py:337
  113.2 9.2 %mix_x.6 = f32[16,6,24,128]{3,2,1,0:T(8,128)} custom-call(f32[16,9,24,128]{3,2,1,0:T(8,128)} %copy-done, bf16[768,256]{1,0:T(8,128)(2,1)} %constant.16.clone.refs_1_.refs_7_, bf16[768,256]{1,0:T(8,128)(2,1)} %constant.17.clone.refs_2_.refs_8_, bf16[2,20,20,48,96]{4,3,2,1,0:T(8,128)(2,1)} %refs_5_.5, bf16[2,20,20,48,96]{4,3,2,1,0:T(8,128)(2,1)} %refs_5_.5, ...), custom_call_target="tpu_custom_call" | custom-call | flops 3840000000 | bytes 2359296 | tf_op jit(solution)/shard_map/mix_x/pallas_call | solution.py:320
  122.4 17.0 %all-to-all-done.4.refs_0_ = f32[16,6,24,128]{3,2,1,0:T(8,128)} async-done(((f32[16,6,24,128]{3,2,1,0:T(8,128)}), f32[16,6,24,128]{3,2,1,0:T(8,128)}, u32[]{:S(2)}, u32[]{:S(2)}) %all-to-all-start.4) | async-done | bytes 1179680 | tf_op jit(solution)/shard_map/all_to_all | solution.py:337
  139.5 6.2 %all-to-all-start.3 = ((f32[16,6,24,128]{3,2,1,0:T(8,128)}), f32[16,6,24,128]{3,2,1,0:T(8,128)}, u32[]{:S(2)}, u32[]{:S(2)}) async-start(f32[16,6,24,128]{3,2,1,0:T(8,128)} %mix_x.6), calls=%async_computation.3 | async-start | bytes 2359296 | tf_op jit(solution)/shard_map/all_to_all | solution.py:337
  145.7 0.1 collective-permute-start.4
  145.8 6.4 %mix_x.5 = f32[16,3,24,128]{3,2,1,0:T(8,128)} custom-call(f32[16,9,24,128]{3,2,1,0:T(8,128)} %copy-done, bf16[768,256]{1,0:T(8,128)(2,1)} %constant.16.clone.refs_1_.refs_7_, bf16[768,256]{1,0:T(8,128)(2,1)} %constant.17.clone.refs_2_.refs_8_, bf16[2,20,20,48,96]{4,3,2,1,0:T(8,128)(2,1)} %refs_5_.5, bf16[2,20,20,48,96]{4,3,2,1,0:T(8,128)(2,1)} %refs_5_.5, ...), custom_call_target="tpu_custom_call" | custom-call | flops 1920000000 | bytes 1179648 | tf_op jit(solution)/shard_map/mix_x/pallas_call | solution.py:320
  152.2 19.4 %all-to-all-done.3.refs_0_ = f32[16,6,24,128]{3,2,1,0:T(8,128)} async-done(((f32[16,6,24,128]{3,2,1,0:T(8,128)}), f32[16,6,24,128]{3,2,1,0:T(8,128)}, u32[]{:S(2)}, u32[]{:S(2)}) %all-to-all-start.3) | async-done | bytes 1179680 | tf_op jit(solution)/shard_map/all_to_all | solution.py:337
  171.6 6.4 %all-to-all-start.2 = ((f32[16,3,24,128]{3,2,1,0:T(8,128)}), f32[16,3,24,128]{3,2,1,0:T(8,128)S(1)}, u32[]{:S(2)}, u32[]{:S(2)}) async-start(f32[16,3,24,128]{3,2,1,0:T(8,128)} %mix_x.5), calls=%async_computation.2 | async-start | bytes 1179648 | tf_op jit(solution)/shard_map/all_to_all | solution.py:337
  178.0 0.1 copy.16
  178.1 0.1 collective-permute-start.3
  178.2 0.4 multiply_convert_fusion
  178.6 1.8 convert_element_type.22.refs_5_
  180.4 13.0 %all-to-all-done.2.refs_0_ = f32[16,3,24,128]{3,2,1,0:T(8,128)S(1)} async-done(((f32[16,3,24,128]{3,2,1,0:T(8,128)}), f32[16,3,24,128]{3,2,1,0:T(8,128)S(1)}, u32[]{:S(2)}, u32[]{:S(2)}) %all-to-all-start.2) | async-done | bytes 589856 | tf_op jit(solution)/shard_map/all_to_all | solution.py:337
  193.4 13.5 %inverse_zy.3.refs_7_ = bf16[20,24,96,128]{3,2,1,0:T(8,128)(2,1)} custom-call(f32[16,6,24,128]{3,2,1,0:T(8,128)} %all-to-all-done.4.refs_0_, f32[16,6,24,128]{3,2,1,0:T(8,128)} %collective-permute-done.4.refs_1_, bf16[20,24,96,128]{3,2,1,0:T(8,128)(2,1)} %bitcast.9, bf16[2,192,256]{2,1,0:T(8,128)(2,1)} %constant.15.clone.refs_3_, ...), custom_call_target="tpu_custom_call" | custom-call | flops 11520000000 | bytes 14155776 | tf_op jit(solution)/shard_map/inverse_zy/pallas_call | solution.py:361
  207.0 13.4 %inverse_zy.4.refs_7_ = bf16[20,24,96,128]{3,2,1,0:T(8,128)(2,1)} custom-call(f32[16,6,24,128]{3,2,1,0:T(8,128)} %all-to-all-done.3.refs_0_, f32[16,6,24,128]{3,2,1,0:T(8,128)} %collective-permute-done.3.refs_1_, bf16[20,24,96,128]{3,2,1,0:T(8,128)(2,1)} %bitcast.10, bf16[2,192,256]{2,1,0:T(8,128)(2,1)} %constant.15.clone.refs_3_, ...), custom_call_target="tpu_custom_call", output_to_operand_aliasing={{}: (7, {})} | custom-call | flops 11520000000 | bytes 14155776 | tf_op jit(solution)/shard_map/inverse_zy/pallas_call | solution.py:361
  220.3 0.8 copy-done.3
  221.2 10.8 %inverse_zy.5 = bf16[20,24,96,128]{3,2,1,0:T(8,128)(2,1)} custom-call(f32[16,3,24,128]{3,2,1,0:T(8,128)} %copy-done.1, f32[16,3,24,128]{3,2,1,0:T(8,128)} %copy-done.3, bf16[20,24,96,128]{3,2,1,0:T(8,128)(2,1)} %bitcast.11, bf16[2,192,256]{2,1,0:T(8,128)(2,1)} %constant.15.clone.refs_3_, ...), custom_call_target="tpu_custom_call", output_to_operand_aliasing={{}: (7, {})} | custom-call | flops 5760000000 | bytes 7077888 | tf_op jit(solution)/shard_map/inverse_zy/pallas_call | solution.py:361
  (14 shorter events, 0.0 us)
Async XLA Ops:
  9.2 3.2 %collective-permute-start.1 = (f32[16,6,24,128]{3,2,1,0:T(8,128)}, f32[16,6,24,128]{3,2,1,0:T(8,128)S(1)}, u32[]{:S(2)}, u32[]{:S(2)}) collective-permute-start(f32[16,6,24,128]{3,2,1,0:T(8,128)} %get-tuple-element.12), channel_id=1, source_target_pairs={{0,1},{1,0},{2,3},{3,2},{4,5},{5,4},{6,7},{7,6},{8,9},{9,8},{10,11... | collective-permute-start | bytes 3538952 | tf_op jit(solution)/shard_map/ppermute | solution.py:281
  14.8 35.3 %all-to-all-start.1 = ((f32[16,6,24,128]{3,2,1,0:T(8,128)}), f32[16,6,24,128]{3,2,1,0:T(8,128)S(1)}, u32[]{:S(2)}, u32[]{:S(2)}) async-start(f32[16,6,24,128]{3,2,1,0:T(8,128)} %add.7), calls=%async_computation.1 | async-start | bytes 2359296 | tf_op jit(solution)/shard_map/all_to_all | solution.py:283
  35.0 3.9 %collective-permute-start = (f32[16,9,24,128]{3,2,1,0:T(8,128)}, f32[16,9,24,128]{3,2,1,0:T(8,128)S(1)}, u32[]{:S(2)}, u32[]{:S(2)}) collective-permute-start(f32[16,9,24,128]{3,2,1,0:T(8,128)} %get-tuple-element.10), channel_id=1, source_target_pairs={{0,1},{1,0},{2,3},{3,2},{4,5},{5,4},{6,7},{7,6},{8,9},{9,8},{10,11... | collective-permute-start | bytes 5308424 | tf_op jit(solution)/shard_map/ppermute | solution.py:281
  50.1 1.0 copy-start.2
  51.2 43.4 %all-to-all-start = ((f32[16,9,24,128]{3,2,1,0:T(8,128)}), f32[16,9,24,128]{3,2,1,0:T(8,128)S(1)}, u32[]{:S(2)}, u32[]{:S(2)}) async-start(f32[16,9,24,128]{3,2,1,0:T(8,128)} %add.6), calls=%async_computation | async-start | bytes 3538944 | tf_op jit(solution)/shard_map/all_to_all | solution.py:283
  94.5 1.2 copy-start
  104.9 34.6 %all-to-all-start.4 = ((f32[16,6,24,128]{3,2,1,0:T(8,128)}), f32[16,6,24,128]{3,2,1,0:T(8,128)}, u32[]{:S(2)}, u32[]{:S(2)}) async-start(f32[16,6,24,128]{3,2,1,0:T(8,128)} %mix_x.7), calls=%async_computation.4 | async-start | bytes 2359296 | tf_op jit(solution)/shard_map/all_to_all | solution.py:337
  139.5 32.2 %all-to-all-start.3 = ((f32[16,6,24,128]{3,2,1,0:T(8,128)}), f32[16,6,24,128]{3,2,1,0:T(8,128)}, u32[]{:S(2)}, u32[]{:S(2)}) async-start(f32[16,6,24,128]{3,2,1,0:T(8,128)} %mix_x.6), calls=%async_computation.3 | async-start | bytes 2359296 | tf_op jit(solution)/shard_map/all_to_all | solution.py:337
  145.7 32.3 %copy-start.4 = (bf16[20,20]{1,0:T(8,128)(2,1)S(1)}, bf16[20,20]{1,0:T(8,128)(2,1)}, u32[]{:S(2)}) copy-start(bf16[20,20]{1,0:T(8,128)(2,1)} %param.14) | copy-start | bytes 2404
  145.7 47.7 %collective-permute-start.4 = (f32[16,6,24,128]{3,2,1,0:T(8,128)}, f32[16,6,24,128]{3,2,1,0:T(8,128)}, u32[]{:S(2)}, u32[]{:S(2)}) collective-permute-start(f32[16,6,24,128]{3,2,1,0:T(8,128)} %all-to-all-done.4.refs_0_), channel_id=1, source_target_pairs={{0,1},{1,0},{2,3},{3,2},{4,5},{5,4},{6,7},{7,6},{8,9},{9,8},{10,11... | collective-permute-start | bytes 3538952 | tf_op jit(solution)/shard_map/ppermute | solution.py:350
  171.6 21.8 %all-to-all-start.2 = ((f32[16,3,24,128]{3,2,1,0:T(8,128)}), f32[16,3,24,128]{3,2,1,0:T(8,128)S(1)}, u32[]{:S(2)}, u32[]{:S(2)}) async-start(f32[16,3,24,128]{3,2,1,0:T(8,128)} %mix_x.5), calls=%async_computation.2 | async-start | bytes 1179648 | tf_op jit(solution)/shard_map/all_to_all | solution.py:337
  178.1 28.9 %collective-permute-start.3 = (f32[16,6,24,128]{3,2,1,0:T(8,128)}, f32[16,6,24,128]{3,2,1,0:T(8,128)}, u32[]{:S(2)}, u32[]{:S(2)}) collective-permute-start(f32[16,6,24,128]{3,2,1,0:T(8,128)} %all-to-all-done.3.refs_0_), channel_id=1, source_target_pairs={{0,1},{1,0},{2,3},{3,2},{4,5},{5,4},{6,7},{7,6},{8,9},{9,8},{10,11... | collective-permute-start | bytes 3538952 | tf_op jit(solution)/shard_map/ppermute | solution.py:350
  193.4 13.5 %copy-start.1 = (f32[16,3,24,128]{3,2,1,0:T(8,128)}, f32[16,3,24,128]{3,2,1,0:T(8,128)S(1)}, u32[]{:S(2)}) copy-start(f32[16,3,24,128]{3,2,1,0:T(8,128)S(1)} %all-to-all-done.2.refs_0_) | copy-start | bytes 1769476
  193.4 26.9 %collective-permute-start.2 = (f32[16,3,24,128]{3,2,1,0:T(8,128)S(1)}, f32[16,3,24,128]{3,2,1,0:T(8,128)S(1)}, u32[]{:S(2)}, u32[]{:S(2)}) collective-permute-start(f32[16,3,24,128]{3,2,1,0:T(8,128)S(1)} %all-to-all-done.2.refs_0_), channel_id=1, source_target_pairs={{0,1},{1,0},{2,3},{3,2},{4,5},{5,4},{6,7},{7,6},{8,9},{9,8},{10,11... | collective-permute-start | bytes 1769480 | tf_op jit(solution)/shard_map/ppermute | solution.py:350
  220.3 0.8 copy-start.3
